TPU v7x, 32 devices: a whole 2x2x4 slice. The times are simulated.
32 devices in a mesh: groups: 2 (over y), rows: 4 (over z), cols: 4 (over x, core).
Axes of the slice: x: 2, y: 2, z: 4, core: 2. Of those that a mesh axis runs over, the one named last changes fastest.
Arguments:
- tokens: bfloat16 [112, 112, 256], P(('groups', 'rows'), 'cols'), parts along dimension 0, may hold values from -6 to 6
- cotangent: bfloat16 [56, 56, 512], P(('groups', 'rows'), 'cols'), parts along dimension 0, may hold values from -6 to 6
- shift_offsets: int32 [4], replicated, may hold values from 1 to 6
- norm2_gain: float32 [256], replicated, may hold values from 0.1 to 1.9
- qkv2: bfloat16 [256, 768], replicated, may hold values from -0.375 to 0.375
- proj2: bfloat16 [256, 256], replicated, may hold values from -0.375 to 0.375
- merge_gain: float32 [1024], replicated, may hold values from 0.1 to 1.9
- merge_weight: bfloat16 [1024, 512], replicated, may hold values from -0.1875 to 0.1875
- norm3_gain: float32 [512], replicated, may hold values from 0.1 to 1.9
- qkv3: bfloat16 [512, 1536], replicated, may hold values from -0.25 to 0.25
- proj3: bfloat16 [512, 512], replicated, may hold values from -0.25 to 0.25
Outputs:
- merged_out: bfloat16 [56, 56, 512], P(('groups', 'rows'), 'cols'), parts along dimension 0
- tokens_grad: bfloat16 [112, 112, 256], P(('groups', 'rows'), 'cols'), parts along dimension 0
- gain_grads: float32 [3584], P('groups'), parts along dimension 0
- qkv2_grad: bfloat16 [393216], P(('groups', 'rows', 'cols')), parts along dimension 0
- proj2_grad: bfloat16 [131072], P(('groups', 'rows', 'cols')), parts along dimension 0
- merge_grad: bfloat16 [1048576], P(('groups', 'rows', 'cols')), parts along dimension 0
- qkv3_grad: bfloat16 [1572864], P(('groups', 'rows', 'cols')), parts along dimension 0
- proj3_grad: bfloat16 [524288], P(('groups', 'rows', 'cols')), parts along dimension 0
There are 2 independent parts, one for each index of `groups`. A program takes and returns all parts, laid end to end along the dimension named above; an argument that names none is the same for every part. Nothing has to cross between parts.
All inputs are finite; a program needn't handle non-finite values.
Results may differ from a plain program's by a relative error of at most 0.033.
Values may be sent and summed in bfloat16 or wider, within the bound.
A program may use at most 128 MiB of HBM per device.

v0:
```python
import jax
import jax.numpy as jnp
from jax import lax
from jax.sharding import PartitionSpec as P

HEADS2 = 8
HEADS3 = 16
WIN = 7


EPSILON = 1e-05
MASKED = -100.0


def passed_along(value, axis, by):
    count = lax.axis_size(axis)
    return lax.ppermute(value, axis, [(i, (i + by) % count) for i in range(count)])


def normalize(inputs, gain):
    widened = inputs.astype(jnp.float32)
    centred = widened - jnp.mean(widened, axis=-1, keepdims=True)
    spread = jnp.mean(centred * centred, axis=-1, keepdims=True)
    return (centred * lax.rsqrt(spread + EPSILON) * gain).astype(jnp.bfloat16)


def attend(packed, heads, region):
    count, window_area, triple = packed.shape
    width = triple // 3
    head_size = width // heads
    queries = packed[:, :, :width].astype(jnp.float32).reshape(count, window_area, heads, head_size)
    key_part = (
        packed[:, :, width : 2 * width]
        .astype(jnp.float32)
        .reshape(count, window_area, heads, head_size)
    )
    values = (
        packed[:, :, 2 * width :].astype(jnp.float32).reshape(count, window_area, heads, head_size)
    )
    scores = jnp.einsum("nphd,nqhd->nhpq", queries, key_part) * head_size ** (-0.5)
    scores = scores + region[:, None, :, :]
    raised = jnp.exp(scores)
    weights = (raised / jnp.sum(raised, axis=-1, keepdims=True)).astype(jnp.bfloat16)
    mixed = jnp.einsum("nhpq,nqhd->nphd", weights.astype(jnp.float32), values)
    return mixed.reshape(count, window_area, width).astype(jnp.bfloat16)


def to_windows(values, window):
    height, breadth, width = values.shape
    shaped = values.reshape(height // window, window, breadth // window, window, width)
    return shaped.transpose(0, 2, 1, 3, 4).reshape(-1, window * window, width)


def from_windows(windows, height, breadth, window):
    width = windows.shape[-1]
    shaped = windows.reshape(height // window, breadth // window, window, window, width)
    return shaped.transpose(0, 2, 1, 3, 4).reshape(height, breadth, width)


def pair_join(values):
    height, breadth, width = values.shape
    shaped = values.reshape(height // 2, 2, breadth // 2, 2, width)
    return shaped.transpose(0, 2, 3, 1, 4).reshape(height // 2, breadth // 2, 4 * width)


def pair_split(joined):
    height, breadth, joined_width = joined.shape
    width = joined_width // 4
    shaped = joined.reshape(height, breadth, 2, 2, width)
    return shaped.transpose(0, 3, 1, 2, 4).reshape(2 * height, 2 * breadth, width)


def region_bias(row_coords, col_coords, height, breadth, shift_rows, shift_cols):
    row_label = jnp.where(
        row_coords < height - WIN, 0, jnp.where(row_coords < height - shift_rows, 1, 2)
    )
    col_label = jnp.where(
        col_coords < breadth - WIN, 0, jnp.where(col_coords < breadth - shift_cols, 1, 2)
    )
    labels = (row_label[:, None] * 3 + col_label[None, :]).astype(jnp.int32)
    windowed = to_windows(labels[:, :, None], WIN)[:, :, 0]
    return jnp.where(windowed[:, :, None] == windowed[:, None, :], 0.0, MASKED).astype(jnp.float32)


def keep_same(values):
    return values


def roll_ahead(values, source, convert, send_rows, send_cols, shift_rows, shift_cols):
    margin = WIN - 1
    received = send_rows(source[:margin])
    taller = jnp.concatenate([values, convert(received)], axis=0)
    moved = lax.dynamic_slice_in_dim(taller, shift_rows, values.shape[0], 0)
    strip = jnp.concatenate([source[:, :margin], received[:, :margin]], axis=0)
    strip = lax.dynamic_slice_in_dim(strip, shift_rows, values.shape[0], 0)
    beside = convert(send_cols(strip))
    wider = jnp.concatenate([moved, beside], axis=1)
    return lax.dynamic_slice_in_dim(wider, shift_cols, values.shape[1], 1)


def roll_behind(values, send_rows, send_cols, shift_rows, shift_cols):
    margin = WIN - 1
    above = send_rows(values[-margin:])
    taller = jnp.concatenate([above, values], axis=0)
    moved = lax.dynamic_slice_in_dim(taller, margin - shift_rows, values.shape[0], 0)
    beside = send_cols(moved[:, -margin:])
    wider = jnp.concatenate([beside, moved], axis=1)
    return lax.dynamic_slice_in_dim(wider, margin - shift_cols, values.shape[1], 1)


def ahead_two_rows(piece):
    return passed_along(piece, "rows", -1)


def ahead_two_cols(piece):
    return passed_along(piece, "cols", -1)


def behind_two_rows(piece):
    return passed_along(piece, "rows", 1)


def behind_two_cols(piece):
    return passed_along(piece, "cols", 1)


def behind_three_rows(piece):
    return passed_along(piece, "rows", 1)


def behind_three_cols(piece):
    return passed_along(piece, "cols", 1)


def grad_three_rows(piece):
    return passed_along(piece, "rows", -1)


def grad_three_cols(piece):
    return passed_along(piece, "cols", -1)


def on_device(
    tokens,
    cotangent,
    shift_offsets,
    norm2_gain,
    qkv2,
    proj2,
    merge_gain,
    merge_weight,
    norm3_gain,
    qkv3,
    proj3,
):
    tile_rows, tile_cols, narrow = tokens.shape
    wide_width = qkv3.shape[0]
    window_area = WIN * WIN
    height = tile_rows * lax.axis_size("rows")
    breadth = tile_cols * lax.axis_size("cols")
    merged_rows = tile_rows // 2
    merged_cols = tile_cols // 2
    shift_rows = shift_offsets[0]
    shift_cols = shift_offsets[1]
    shift_rows3 = shift_offsets[2]
    shift_cols3 = shift_offsets[3]
    row_coords = lax.axis_index("rows") * tile_rows + jnp.arange(tile_rows, dtype=jnp.int32)
    col_coords = lax.axis_index("cols") * tile_cols + jnp.arange(tile_cols, dtype=jnp.int32)
    bias = region_bias(row_coords, col_coords, height, breadth, shift_rows, shift_cols)
    row_coords3 = lax.axis_index("rows") * merged_rows + jnp.arange(merged_rows, dtype=jnp.int32)
    col_coords3 = lax.axis_index("cols") * merged_cols + jnp.arange(merged_cols, dtype=jnp.int32)
    bias_three = region_bias(
        row_coords3, col_coords3, height // 2, breadth // 2, shift_rows3, shift_cols3
    )
    normed, norm_pull = jax.vjp(normalize, tokens, norm2_gain)
    rolled = to_windows(
        roll_ahead(
            normed, normed, keep_same, ahead_two_rows, ahead_two_cols, shift_rows, shift_cols
        ),
        WIN,
    )
    packed = jnp.dot(rolled.reshape(-1, narrow), qkv2, preferred_element_type=jnp.float32)
    packed = packed.astype(jnp.bfloat16).reshape(rolled.shape[0], window_area, 3 * narrow)
    mixed, mix_pull = jax.vjp(lambda inner: attend(inner, HEADS2, bias), packed)
    projected = jnp.dot(
        mixed.reshape(-1, narrow), proj2, preferred_element_type=jnp.float32
    ).astype(jnp.bfloat16)
    grid = from_windows(projected.reshape(-1, window_area, narrow), tile_rows, tile_cols, WIN)
    restored = roll_behind(grid, behind_two_rows, behind_two_cols, shift_rows, shift_cols)
    section_two = (tokens.astype(jnp.float32) + restored.astype(jnp.float32)).astype(jnp.bfloat16)
    merged_norm, merge_pull = jax.vjp(normalize, pair_join(section_two), merge_gain)
    product = jnp.dot(
        merged_norm.reshape(-1, 4 * narrow), merge_weight, preferred_element_type=jnp.float32
    )
    merged = product.astype(jnp.bfloat16).reshape(merged_norm.shape[:2] + (wide_width,))
    normed_three, norm_three_pull = jax.vjp(normalize, merged, norm3_gain)

    def ahead_three_rows(piece):
        return passed_along(piece, "rows", -1)

    def ahead_three_cols(piece):
        return passed_along(piece, "cols", -1)

    shifted_three = roll_ahead(
        normed_three,
        normed_three,
        keep_same,
        ahead_three_rows,
        ahead_three_cols,
        shift_rows3,
        shift_cols3,
    )
    rolled_three = to_windows(shifted_three, WIN)
    packed_three = jnp.dot(
        rolled_three.reshape(-1, wide_width), qkv3, preferred_element_type=jnp.float32
    )
    packed_three = packed_three.astype(jnp.bfloat16).reshape(
        rolled_three.shape[0], window_area, 3 * wide_width
    )
    mixed_three, mix_three_pull = jax.vjp(
        lambda inner: attend(inner, HEADS3, bias_three), packed_three
    )
    projected_three = jnp.dot(
        mixed_three.reshape(-1, wide_width), proj3, preferred_element_type=jnp.float32
    ).astype(jnp.bfloat16)
    grid_three = from_windows(
        projected_three.reshape(-1, window_area, wide_width), merged_rows, merged_cols, WIN
    )
    restored_three = roll_behind(
        grid_three, behind_three_rows, behind_three_cols, shift_rows3, shift_cols3
    )
    merged_out = (merged.astype(jnp.float32) + restored_three.astype(jnp.float32)).astype(
        jnp.bfloat16
    )
    d_shifted_out = roll_ahead(
        cotangent, cotangent, keep_same, grad_three_rows, grad_three_cols, shift_rows3, shift_cols3
    )
    d_projected_three = to_windows(d_shifted_out, WIN).reshape(-1, wide_width)
    grad_proj3 = jnp.dot(
        mixed_three.reshape(-1, wide_width).T, d_projected_three, preferred_element_type=jnp.float32
    )
    d_mixed_three = jnp.dot(d_projected_three, proj3.T, preferred_element_type=jnp.float32).astype(
        jnp.bfloat16
    )
    (d_packed_three,) = mix_three_pull(d_mixed_three.reshape(mixed_three.shape))
    d_packed_rows = d_packed_three.reshape(-1, 3 * wide_width)
    grad_qkv3 = jnp.dot(
        rolled_three.reshape(-1, wide_width).T, d_packed_rows, preferred_element_type=jnp.float32
    )
    d_rolled_three = jnp.dot(d_packed_rows, qkv3.T, preferred_element_type=jnp.float32).astype(
        jnp.bfloat16
    )
    d_normed_three = roll_behind(
        from_windows(d_rolled_three.reshape(rolled_three.shape), merged_rows, merged_cols, WIN),
        behind_three_rows,
        behind_three_cols,
        shift_rows3,
        shift_cols3,
    )
    d_merged_norm, grad_gain_three = norm_three_pull(d_normed_three)
    d_merged_rows = (cotangent + d_merged_norm).reshape(-1, wide_width)
    grad_merge = jnp.dot(
        merged_norm.reshape(-1, 4 * narrow).T, d_merged_rows, preferred_element_type=jnp.float32
    )
    d_joined_norm = jnp.dot(d_merged_rows, merge_weight.T, preferred_element_type=jnp.float32)
    d_joined_norm = d_joined_norm.astype(jnp.bfloat16).reshape(merged_norm.shape)
    d_joined, grad_gain_merge = merge_pull(d_joined_norm)
    d_section_two = pair_split(d_joined)
    d_projected = to_windows(
        roll_ahead(
            d_section_two,
            d_section_two,
            keep_same,
            ahead_two_rows,
            ahead_two_cols,
            shift_rows,
            shift_cols,
        ),
        WIN,
    ).reshape(-1, narrow)
    grad_proj2 = jnp.dot(
        mixed.reshape(-1, narrow).T, d_projected, preferred_element_type=jnp.float32
    )
    d_mixed = jnp.dot(d_projected, proj2.T, preferred_element_type=jnp.float32).astype(jnp.bfloat16)
    (d_packed,) = mix_pull(d_mixed.reshape(mixed.shape))
    d_packed_two = d_packed.reshape(-1, 3 * narrow)
    grad_qkv2 = jnp.dot(
        rolled.reshape(-1, narrow).T, d_packed_two, preferred_element_type=jnp.float32
    )
    d_rolled = jnp.dot(d_packed_two, qkv2.T, preferred_element_type=jnp.float32).astype(
        jnp.bfloat16
    )
    d_normed = roll_behind(
        from_windows(d_rolled.reshape(rolled.shape), tile_rows, tile_cols, WIN),
        behind_two_rows,
        behind_two_cols,
        shift_rows,
        shift_cols,
    )
    d_tokens_norm, grad_gain_two = norm_pull(d_normed)
    tokens_grad = d_section_two + d_tokens_norm
    summed = (
        lax.psum_scatter(grad_qkv2.reshape(-1), ("rows", "cols"), scatter_dimension=0, tiled=True),
        lax.psum_scatter(grad_proj2.reshape(-1), ("rows", "cols"), scatter_dimension=0, tiled=True),
        lax.psum_scatter(grad_merge.reshape(-1), ("rows", "cols"), scatter_dimension=0, tiled=True),
        lax.psum_scatter(grad_qkv3.reshape(-1), ("rows", "cols"), scatter_dimension=0, tiled=True),
        lax.psum_scatter(grad_proj3.reshape(-1), ("rows", "cols"), scatter_dimension=0, tiled=True),
    )
    gains = lax.psum(
        jnp.concatenate([grad_gain_two, grad_gain_merge, grad_gain_three]), ("rows", "cols")
    )
    return (
        merged_out,
        tokens_grad,
        gains,
        summed[0].astype(jnp.bfloat16),
        summed[1].astype(jnp.bfloat16),
        summed[2].astype(jnp.bfloat16),
        summed[3].astype(jnp.bfloat16),
        summed[4].astype(jnp.bfloat16),
    )


def solution(mesh):
    in_specs = (
        P(("groups", "rows"), "cols", None),
        P(("groups", "rows"), "cols", None),
        P(),
        P(),
        P(),
        P(),
        P(),
        P(),
        P(),
        P(),
        P(),
    )
    out_specs = (
        P(("groups", "rows"), "cols", None),
        P(("groups", "rows"), "cols", None),
        P("groups"),
        P(("groups", "rows", "cols")),
        P(("groups", "rows", "cols")),
        P(("groups", "rows", "cols")),
        P(("groups", "rows", "cols")),
        P(("groups", "rows", "cols")),
    )
    return jax.shard_map(
        on_device, mesh=mesh, in_specs=in_specs, out_specs=out_specs, check_vma=False
    )
```

profile of v0, /device:TPU:0, one launch (start us, length us, event | category | flops | bytes accessed | tf_op | source)
XLA Modules:
  0.0 384.1 jit_solution(11638216400509128212)
XLA Ops:
  4.8 5.1 %collective-permute-start = (bf16[6,28,256]{2,1,0:T(8,128)(2,1)S(1)}, bf16[6,28,256]{2,1,0:T(8,128)(2,1)S(1)}, u32[]{:S(2)}, u32[]{:S(2)}) collective-permute-start(bf16[6,28,256]{2,1,0:T(8,128)(2,1)S(1)} %slice.132), channel_id=1, source_target_pairs={{0,12},{4,0},{8,4},{12,8},{1,13},{5,1},{9,5},{13,9},{2,14},{6,2},{... | collective-permute-start | bytes 258056 | tf_op jit(solution)/shard_map/ppermute | solution.py:17
  21.2 1.7 collective-permute-done.1
  27.6 1.9 fusion.81
  32.3 1.6 collective-permute-start.2
  56.3 2.1 reshape.407
  59.0 2.7 fusion.82
  63.4 1.6 multiply_reduce_fusion.4
  69.3 2.2 collective-permute-start.4
  74.4 2.1 reshape.410
  78.8 1.9 fusion.58
  82.2 1.6 reshape_reshape.30
  83.8 2.0 convolution_convert_fusion.18
  85.9 1.7 copy.243
  87.5 1.7 reshape.393
  92.5 2.0 convolution_convert_fusion
  94.5 1.8 reshape.387
  96.2 1.7 fusion.79
  98.0 1.8 copy.232
  99.7 1.8 copy.231
  101.5 2.4 fusion.83
  104.5 1.8 copy.230
  106.3 1.9 multiply_reduce_fusion
  111.4 1.8 copy.251
  113.1 1.8 copy.249
  114.9 1.8 copy.246
  116.6 1.8 pad_add_fusion.1
  118.4 1.8 reshape.394
  120.2 2.2 convolution_convert_fusion.17
  122.4 1.6 reshape_reshape.31
  125.5 1.6 copy.254
  129.6 1.8 convert_element_type.273
  131.4 2.0 convolution_convert_fusion.19
  133.4 1.6 reshape_reshape.29
  135.9 1.6 copy.236
  137.5 3.3 fusion.85
  143.7 4.4 %reshape.405 = f32[786432]{0:T(1024)} reshape(f32[512,1536]{1,0:T(8,128)} %fusion.85) | data formatting | bytes 6291456 | tf_op jit(solution)/shard_map/reshape | solution.py:306
  157.8 2.3 fusion.34
  166.9 3.6 collective-permute-start.12
  170.6 2.9 convolution_bitcast_fusion
  174.4 3.5 copy.288
  178.4 1.7 collective-permute-done.13
  183.5 2.4 fusion.4
  195.4 1.6 copy.273
  197.1 1.7 reshape.401
  201.1 5.9 %collective-permute-done.14 = bf16[6,28,256]{2,1,0:T(8,128)(2,1)S(1)} collective-permute-done((bf16[6,28,256]{2,1,0:T(8,128)(2,1)S(1)}, bf16[6,28,256]{2,1,0:T(8,128)(2,1)S(1)}, u32[]{:S(2)}, u32[]{:S(2)}) %collective-permute-start.14) | collective-permute-done | bytes 86048 | tf_op jit(solution)/shard_map/ppermute | solution.py:17
  208.2 2.2 reshape.402
  210.4 1.8 copy.287
  216.1 162.4 %all-reduce.13 = (f32[1792]{0:T(1024)}, bf16[196608]{0:T(1024)(128)(2,1)}, bf16[65536]{0:T(1024)(128)(2,1)S(1)}, bf16[524288]{0:T(1024)(128)(2,1)}, bf16[786432]...) all-reduce(f32[1792]{0:T(1024)S(1)} %pad_maximum_fusion, ...), channel_id=1, replica_groups=mesh['groups'=2,'rows'=4,'cols'=4] {'rows','cols'}, use_global_device_ids=true, to_apply=%region_19.20 | all-reduce | flops 1836800 | bytes 11024384 | tf_op jit(solution)/shard_map/psum | solution.py:309
  (316 shorter events, 97.5 us)
Async XLA Ops:
  0.6 91.8 %copy-start = (bf16[512,1536]{1,0:T(8,128)(2,1)S(1)}, bf16[512,1536]{1,0:T(8,128)(2,1)}, u32[]{:S(2)}) copy-start(bf16[512,1536]{1,0:T(8,128)(2,1)} %param.20) | copy-start | bytes 4718596
  1.9 9.1 %copy-start.36 = (f32[14,28]{1,0:T(8,128)}, f32[14,28]{1,0:T(8,128)S(1)}, u32[]{:S(2)}) copy-start(f32[14,28]{1,0:T(8,128)S(1)} %broadcast_multiply_fusion) | copy-start | bytes 4708
  3.7 7.3 %copy-start.41 = (f32[14,28]{1,0:T(8,128)}, f32[14,28]{1,0:T(8,128)S(1)}, u32[]{:S(2)}) copy-start(f32[14,28]{1,0:T(8,128)S(1)} %fusion.66) | copy-start | bytes 4708
  4.8 18.5 %copy-start.21 = (bf16[256,768]{1,0:T(8,128)(2,1)S(1)}, bf16[256,768]{1,0:T(8,128)(2,1)}, u32[]{:S(2)}) copy-start(bf16[256,768]{1,0:T(8,128)(2,1)} %param.15) | copy-start | bytes 1179652
  4.8 15.7 %collective-permute-start = (bf16[6,28,256]{2,1,0:T(8,128)(2,1)S(1)}, bf16[6,28,256]{2,1,0:T(8,128)(2,1)S(1)}, u32[]{:S(2)}, u32[]{:S(2)}) collective-permute-start(bf16[6,28,256]{2,1,0:T(8,128)(2,1)S(1)} %slice.132), channel_id=1, source_target_pairs={{0,12},{4,0},{8,4},{12,8},{1,13},{5,1},{9,5},{13,9},{2,14},{6,2},{... | collective-permute-start | bytes 258056 | tf_op jit(solution)/shard_map/ppermute | solution.py:17
  10.9 28.9 %copy-start.26 = (bf16[7,14,512]{2,0,1:T(8,128)(2,1)}, bf16[7,14,512]{2,0,1:T(8,128)(2,1)S(1)}, u32[]{:S(2)}) copy-start(bf16[7,14,512]{2,0,1:T(8,128)(2,1)S(1)} %copy.259) | copy-start | bytes 301060
  11.0 36.6 %collective-permute-start.8 = (bf16[6,14,512]{2,0,1:T(8,128)(2,1)S(1)}, bf16[6,14,512]{2,0,1:T(8,128)(2,1)}, u32[]{:S(2)}, u32[]{:S(2)}) collective-permute-start(bf16[6,14,512]{2,0,1:T(8,128)(2,1)S(1)} %bitcast.165), channel_id=1, source_target_pairs={{0,12},{4,0},{8,4},{12,8},{1,13},{5,1},{9,5},{13,9},{2,14},{6,2},{... | collective-permute-start | bytes 258056 | tf_op jit(solution)/shard_map/ppermute | solution.py:17
  20.7 2.3 collective-permute-start.1
  30.9 10.9 %copy-start.49 = (f32[1024]{0:T(1024)S(1)}, f32[1024]{0:T(1024)}, u32[]{:S(2)}) copy-start(f32[1024]{0:T(1024)} %param.17) | copy-start | bytes 12292
  30.9 11.5 %copy-start.65 = (u32[32]{0:T(128)S(1)}, u32[32]{0:T(128)}, u32[]{:S(2)}) copy-start(u32[32]{0:T(128)} %constant.102) | copy-start | bytes 388
  31.8 20.3 %copy-start.9 = (bf16[392,256]{0,1:T(8,128)(2,1)}, bf16[392,256]{0,1:T(8,128)(2,1)S(1)}, u32[]{:S(2)}) copy-start(bf16[392,256]{0,1:T(8,128)(2,1)S(1)} %convert_element_type.254) | copy-start | bytes 602116
  31.8 20.3 %copy-start.1 = (bf16[14,28,256]{2,1,0:T(8,128)(2,1)S(1)}, bf16[14,28,256]{2,1,0:T(8,128)(2,1)}, u32[]{:S(2)}) copy-start(bf16[14,28,256]{2,1,0:T(8,128)(2,1)} %param.11) | copy-start | bytes 602116
  32.3 16.1 %collective-permute-start.2 = (bf16[6,28,256]{2,1,0:T(8,128)(2,1)S(1)}, bf16[6,28,256]{2,1,0:T(8,128)(2,1)S(1)}, u32[]{:S(2)}, u32[]{:S(2)}) collective-permute-start(bf16[6,28,256]{2,1,0:T(8,128)(2,1)S(1)} %slice.138), channel_id=1, source_target_pairs={{0,4},{4,8},{8,12},{12,0},{1,5},{5,9},{9,13},{13,1},{2,6},{6,10},{... | collective-permute-start | bytes 258056 | tf_op jit(solution)/shard_map/ppermute | solution.py:17
  48.5 3.7 collective-permute-start.3
  50.2 30.5 %collective-permute-start.9 = (bf16[7,6,512]{2,0,1:T(8,128)(2,1)}, bf16[7,6,512]{2,0,1:T(8,128)(2,1)}, u32[]{:S(2)}, u32[]{:S(2)}) collective-permute-start(bf16[7,6,512]{2,0,1:T(8,128)(2,1)} %fusion.64), channel_id=1, source_target_pairs={{0,3},{1,0},{2,1},{3,2},{4,7},{5,4},{6,5},{7,6},{8,11},{9,8},{10,9... | collective-permute-start | bytes 129032 | tf_op jit(solution)/shard_map/ppermute | solution.py:17
  53.0 6.0 %copy-start.4 = (bf16[1024,512]{1,0:T(8,128)(2,1)S(1)}, bf16[1024,512]{1,0:T(8,128)(2,1)}, u32[]{:S(2)}) copy-start(bf16[1024,512]{1,0:T(8,128)(2,1)} %param.18) | copy-start | bytes 3145732
  55.7 7.8 %copy-start.43 = (f32[7,14]{1,0:T(8,128)}, f32[7,14]{1,0:T(8,128)S(1)}, u32[]{:S(2)}) copy-start(f32[7,14]{1,0:T(8,128)S(1)} %broadcast_multiply_fusion.1) | copy-start | bytes 1180
  56.2 7.3 %copy-start.52 = (f32[7,14]{1,0:T(8,128)}, f32[7,14]{1,0:T(8,128)S(1)}, u32[]{:S(2)}) copy-start(f32[7,14]{1,0:T(8,128)S(1)} %multiply_reduce_fusion.3) | copy-start | bytes 1180
  56.2 5.5 %copy-start.59 = (f32[98]{0:T(128)}, f32[98]{0:T(128)S(1)}, u32[]{:S(2)}) copy-start(f32[98]{0:T(128)S(1)} %div.114) | copy-start | bytes 1180
  69.3 7.2 %collective-permute-start.4 = (bf16[6,14,512]{2,0,1:T(8,128)(2,1)}, bf16[6,14,512]{2,0,1:T(8,128)(2,1)}, u32[]{:S(2)}, u32[]{:S(2)}) collective-permute-start(bf16[6,14,512]{2,0,1:T(8,128)(2,1)} %bitcast.135), channel_id=1, source_target_pairs={{0,12},{4,0},{8,4},{12,8},{1,13},{5,1},{9,5},{13,9},{2,14},{6,2},{... | collective-permute-start | bytes 258056 | tf_op jit(solution)/shard_map/ppermute | solution.py:17
  78.8 10.5 %collective-permute-start.5 = (bf16[7,6,512]{2,0,1:T(8,128)(2,1)}, bf16[7,6,512]{2,0,1:T(8,128)(2,1)}, u32[]{:S(2)}, u32[]{:S(2)}) collective-permute-start(bf16[7,6,512]{2,0,1:T(8,128)(2,1)} %fusion.65), channel_id=1, source_target_pairs={{0,3},{1,0},{2,1},{3,2},{4,7},{5,4},{6,5},{7,6},{8,11},{9,8},{10,9... | collective-permute-start | bytes 129032 | tf_op jit(solution)/shard_map/ppermute | solution.py:17
  141.5 9.1 %collective-permute-start.10 = (bf16[6,14,512]{2,0,1:T(8,128)(2,1)}, bf16[6,14,512]{2,0,1:T(8,128)(2,1)}, u32[]{:S(2)}, u32[]{:S(2)}) collective-permute-start(bf16[6,14,512]{2,0,1:T(8,128)(2,1)} %bitcast.31), channel_id=1, source_target_pairs={{0,4},{4,8},{8,12},{12,0},{1,5},{5,9},{9,13},{13,1},{2,6},{6,10},{... | collective-permute-start | bytes 258056 | tf_op jit(solution)/shard_map/ppermute | solution.py:17
  143.7 8.5 %collective-permute-start.6 = (bf16[6,14,512]{2,1,0:T(8,128)(2,1)}, bf16[6,14,512]{2,1,0:T(8,128)(2,1)}, u32[]{:S(2)}, u32[]{:S(2)}) collective-permute-start(bf16[6,14,512]{2,1,0:T(8,128)(2,1)} %slice.118), channel_id=1, source_target_pairs={{0,4},{4,8},{8,12},{12,0},{1,5},{5,9},{9,13},{13,1},{2,6},{6,10},{... | collective-permute-start | bytes 258056 | tf_op jit(solution)/shard_map/ppermute | solution.py:17
  148.1 5.1 %copy-start.33 = (bf16[1,7,2,7,512]{4,1,3,2,0:T(8,128)(2,1)S(1)}, bf16[1,7,2,7,512]{4,1,3,2,0:T(8,128)(2,1)}, u32[]{:S(2)}) copy-start(bf16[1,7,2,7,512]{4,1,3,2,0:T(8,128)(2,1)} %copy.236) | copy-start | bytes 301060
  149.3 5.9 %copy-start.56 = (f32[512]{0:T(512)S(1)}, f32[512]{0:T(512)}, u32[]{:S(2)}) copy-start(f32[512]{0:T(512)} %param.19) | copy-start | bytes 6148
  149.3 8.1 %copy-start.55 = (f32[7,14]{1,0:T(8,128)S(1)}, f32[7,14]{1,0:T(8,128)}, u32[]{:S(2)}) copy-start(f32[7,14]{1,0:T(8,128)} %copy-done.54) | copy-start | bytes 1180
  151.6 3.6 collective-permute-start.11
  154.0 3.8 collective-permute-start.7
  160.1 4.8 %copy-start.44 = (f32[7,14]{1,0:T(8,128)S(1)}, f32[7,14]{1,0:T(8,128)}, u32[]{:S(2)}) copy-start(f32[7,14]{1,0:T(8,128)} %copy-done.43) | copy-start | bytes 1180
  160.1 4.8 %copy-start.48 = (f32[7,14]{1,0:T(8,128)S(1)}, f32[7,14]{1,0:T(8,128)}, u32[]{:S(2)}) copy-start(f32[7,14]{1,0:T(8,128)} %get-tuple-element.63) | copy-start | bytes 1180
  160.1 4.8 %copy-start.51 = (f32[2,2,256]{2,1,0:T(2,128)S(1)}, f32[2,2,256]{2,1,0:T(2,128)}, u32[]{:S(2)}) copy-start(f32[2,2,256]{2,1,0:T(2,128)} %mul.323) | copy-start | bytes 12292
  162.2 3.7 copy-start.62
  166.9 6.7 %copy-start.32 = (bf16[7,14,512]{2,0,1:T(8,128)(2,1)S(1)}, bf16[7,14,512]{2,0,1:T(8,128)(2,1)}, u32[]{:S(2)}) copy-start(bf16[7,14,512]{2,0,1:T(8,128)(2,1)} %get-tuple-element.62) | copy-start | bytes 301060
  166.9 11.0 %collective-permute-start.12 = (bf16[6,28,256]{2,1,0:T(8,128)(2,1)S(1)}, bf16[6,28,256]{2,1,0:T(8,128)(2,1)S(1)}, u32[]{:S(2)}, u32[]{:S(2)}) collective-permute-start(bf16[6,28,256]{2,1,0:T(8,128)(2,1)S(1)} %slice.127), channel_id=1, source_target_pairs={{0,12},{4,0},{8,4},{12,8},{1,13},{5,1},{9,5},{13,9},{2,14},{6,2},{... | collective-permute-start | bytes 258056 | tf_op jit(solution)/shard_map/ppermute | solution.py:17
  178.0 2.1 collective-permute-start.13
  178.4 5.1 %copy-start.16 = (bf16[8,49,256]{1,2,0:T(8,128)(2,1)S(1)}, bf16[8,49,256]{1,2,0:T(8,128)(2,1)}, u32[]{:S(2)}) copy-start(bf16[8,49,256]{1,2,0:T(8,128)(2,1)} %copy-done.15) | copy-start | bytes 602116
  178.4 5.1 %copy-start.40 = (f32[8,8,49]{2,1,0:T(8,128)S(1)}, f32[8,8,49]{2,1,0:T(8,128)}, u32[]{:S(2)}) copy-start(f32[8,8,49]{2,1,0:T(8,128)} %multiply_divide_fusion) | copy-start | bytes 37636
  193.1 6.7 %copy-start.18 = (bf16[392,256]{1,0:T(8,128)(2,1)S(1)}, bf16[392,256]{1,0:T(8,128)(2,1)}, u32[]{:S(2)}) copy-start(bf16[392,256]{1,0:T(8,128)(2,1)} %copy-done.17) | copy-start | bytes 602116
  194.7 12.5 %copy-start.10 = (bf16[392,256]{0,1:T(8,128)(2,1)S(1)}, bf16[392,256]{0,1:T(8,128)(2,1)}, u32[]{:S(2)}) copy-start(bf16[392,256]{0,1:T(8,128)(2,1)} %copy-done.9) | copy-start | bytes 602116
  194.7 12.5 %copy-start.20 = (bf16[392,256]{1,0:T(8,128)(2,1)S(1)}, bf16[392,256]{1,0:T(8,128)(2,1)}, u32[]{:S(2)}) copy-start(bf16[392,256]{1,0:T(8,128)(2,1)} %copy-done.19) | copy-start | bytes 602116
  198.8 8.1 %copy-start.22 = (bf16[14,28,256]{2,1,0:T(8,128)(2,1)S(1)}, bf16[14,28,256]{2,1,0:T(8,128)(2,1)}, u32[]{:S(2)}) copy-start(bf16[14,28,256]{2,1,0:T(8,128)(2,1)} %reshape.401) | copy-start | bytes 602116
  199.8 7.2 %collective-permute-start.14 = (bf16[6,28,256]{2,1,0:T(8,128)(2,1)S(1)}, bf16[6,28,256]{2,1,0:T(8,128)(2,1)S(1)}, u32[]{:S(2)}, u32[]{:S(2)}) collective-permute-start(bf16[6,28,256]{2,1,0:T(8,128)(2,1)S(1)} %slice.156), channel_id=1, source_target_pairs={{0,4},{4,8},{8,12},{12,0},{1,5},{5,9},{9,13},{13,1},{2,6},{6,10},{... | collective-permute-start | bytes 258056 | tf_op jit(solution)/shard_map/ppermute | solution.py:17
  201.1 11.1 %copy-start.37 = (f32[14,28]{1,0:T(8,128)S(1)}, f32[14,28]{1,0:T(8,128)}, u32[]{:S(2)}) copy-start(f32[14,28]{1,0:T(8,128)} %copy-done.36) | copy-start | bytes 4708
  201.1 11.1 %copy-start.57 = (f32[256]{0:T(256)S(1)}, f32[256]{0:T(256)}, u32[]{:S(2)}) copy-start(f32[256]{0:T(256)} %param.14) | copy-start | bytes 3076
  207.0 5.2 %collective-permute-start.15 = (bf16[14,6,256]{2,1,0:T(8,128)(2,1)S(1)}, bf16[14,6,256]{2,1,0:T(8,128)(2,1)}, u32[]{:S(2)}, u32[]{:S(2)}) collective-permute-start(bf16[14,6,256]{2,1,0:T(8,128)(2,1)S(1)} %slice.157), channel_id=1, source_target_pairs={{0,1},{1,2},{2,3},{3,0},{4,5},{5,6},{6,7},{7,4},{8,9},{9,10},{10,1... | collective-permute-start | bytes 129032 | tf_op jit(solution)/shard_map/ppermute | solution.py:17
  208.2 8.0 %copy-start.5 = (f32[64,4,8,128]{3,1,2,0:T(4,128)S(1)}, f32[64,4,8,128]{3,1,2,0:T(4,128)}, u32[]{:S(2)}) copy-start(f32[64,4,8,128]{3,1,2,0:T(4,128)} %copy.289) | copy-start | bytes 3145732
  210.4 4.8 %copy-start.42 = (f32[14,28]{1,0:T(8,128)S(1)}, f32[14,28]{1,0:T(8,128)}, u32[]{:S(2)}) copy-start(f32[14,28]{1,0:T(8,128)} %copy-done.41) | copy-start | bytes 4708
  210.4 5.8 %copy-start.58 = (f32[512]{0:T(512)S(1)}, f32[512]{0:T(512)}, u32[]{:S(2)}) copy-start(f32[512]{0:T(512)} %get-tuple-element.44) | copy-start | bytes 6148
  (34 other events, 74.7 us)
where the time goes:
time: 388 us; the launch traced here: 384 us
  blocking collectives  162 us (42%)
  local copies, waits for them, and re-layouts  98.1 us (25%)
  matrix products  41.8 us (11%)
  other arithmetic  32.8 us (8%)
  between operations  20.6 us (5%)
  starting transfers between devices  17.1 us (4%)
  waiting for transfers between devices  11.3 us (3%)
    psum x1, blocking collectives, on_device(): lax.psum(jnp.concatenate([grad_gain_two, grad_gain_merge, grad_gain_three...  162 us
    unnamed x144, local copies, waits for them, and re-layouts  18.5 us
    ppermute x16, starting transfers between devices, passed_along(): lax.ppermute(value, axis, [(i, (i + by) % count) for i in range(count)])  17.1 us
    ppermute x16, waiting for transfers between devices, passed_along(): lax.ppermute(value, axis, [(i, (i + by) % count) for i in range(count)])  11.3 us
    dot_general x6, matrix products, attend(): jnp.einsum('nphd,nqhd->nhpq', queries, key_part) * head_size ** (-0.5)  9.14 us
    dot_general x6, matrix products, attend(): mixed = jnp.einsum('nhpq,nqhd->nphd', weights.astype(jnp.float32), values)  8.66 us
  transfers between devices with their start and end apart: 16, of which 6 were waited for; matrix products, arithmetic and copies ran while one was open for 20% of the time, Pallas kernels for 0%

commit v1 on v0

v1 whole, which is shorter than its diff:
```python
import functools

import jax
import jax.numpy as jnp
import numpy as np
from jax import lax
from jax.experimental import pallas as pl
from jax.experimental.pallas import tpu as pltpu
from jax.sharding import PartitionSpec as P

HEAD = 32
WIN = 7
MARGIN = WIN - 1
SLOT = 64
PM = 16
LANES = 128
EPSILON = 1e-05
MASKED = -100.0
F32 = jnp.float32
BF16 = jnp.bfloat16


def pitch_of(count):
    return -(-count // 16) * 16


def window_tokens(rows, cols):
    h, w, ok = [], [], []
    for wr in range(rows // WIN):
        for wc in range(cols // WIN):
            for t in range(SLOT):
                good = t < WIN * WIN
                h.append(wr * WIN + t // WIN if good else 0)
                w.append(wc * WIN + t % WIN if good else 0)
                ok.append(good)
    return np.array(h, np.int32), np.array(w, np.int32), np.array(ok)


def grid_tokens(rows, cols, pitch):
    h = np.repeat(np.arange(rows, dtype=np.int32), pitch)
    w = np.tile(np.arange(pitch, dtype=np.int32), rows)
    ok = w < cols
    return h, np.where(ok, w, 0).astype(np.int32), ok


def quad_tokens(rows, cols):
    a, b, ok = grid_tokens(rows // 2, cols // 2, pitch_of(cols // 2))
    h = np.concatenate([2 * a + (k & 1) for k in range(4)])
    w = np.concatenate([2 * b + (k >> 1) for k in range(4)])
    return h, w, np.tile(ok, 4)


def win_index(h, w, cols):
    return ((h // WIN) * (cols // WIN) + w // WIN) * SLOT + (h % WIN) * WIN + w % WIN


def quad_index(h, w, rows, cols):
    pitch = pitch_of(cols // 2)
    return ((h % 2) + 2 * (w % 2)) * ((rows // 2) * pitch) + (h // 2) * pitch + w // 2


def ahead_index(h, w, ok, shift_rows, shift_cols, rows, cols, inner, base):
    pitch = pitch_of(cols)
    h2, w2 = h + shift_rows, w + shift_cols
    local = inner(jnp.minimum(h2, rows - 1), jnp.minimum(w2, cols - 1))
    below = base + (h2 - rows) * pitch + w2
    side = base + MARGIN * pitch + h2 * PM + (w2 - cols)
    idx = jnp.where(w2 >= cols, side, jnp.where(h2 >= rows, below, local))
    return jnp.where(ok, idx, -1).astype(jnp.int32).reshape(-1, 1)


def behind_index(h, w, ok, shift_rows, shift_cols, rows, cols, base):
    pitch = pitch_of(cols)
    h2, w2 = h - shift_rows, w - shift_cols
    local = win_index(jnp.maximum(h2, 0), jnp.maximum(w2, 0), cols)
    above = base + (h2 + MARGIN) * pitch + w2
    row = jnp.where(h2 >= 0, h2, rows + h2 + MARGIN)
    side = base + MARGIN * pitch + row * PM + (w2 + MARGIN)
    idx = jnp.where(w2 < 0, side, jnp.where(h2 < 0, above, local))
    return jnp.where(ok, idx, -1).astype(jnp.int32).reshape(-1, 1)


def piece_index(rows, cols, inner, first):
    top = 0 if first else rows - MARGIN
    left = 0 if first else cols - MARGIN
    parts = []
    for count, wide, pitch, h0, w0 in (
        (MARGIN, cols, pitch_of(cols), top, 0),
        (rows, MARGIN, PM, 0, left),
        (MARGIN, MARGIN, PM, top, left),
    ):
        h, w, ok = grid_tokens(count, wide, pitch)
        parts.append(np.where(ok, inner(h + h0, w + w0), -1))
    return np.concatenate(parts).astype(np.int32).reshape(-1, 1)


def piece_sizes(rows, cols):
    return MARGIN * pitch_of(cols), rows * PM, MARGIN * PM


def window_labels(rows, cols, axis_row, axis_col, shift_rows, shift_cols):
    h, w, ok = window_tokens(rows, cols)
    height = rows * lax.axis_size("rows")
    breadth = cols * lax.axis_size("cols")
    gh = axis_row * rows + h
    gw = axis_col * cols + w
    lh = jnp.where(gh < height - WIN, 0, jnp.where(gh < height - shift_rows, 1, 2))
    lw = jnp.where(gw < breadth - WIN, 0, jnp.where(gw < breadth - shift_cols, 1, 2))
    flat = jnp.where(ok, lh * 3 + lw, -1).astype(jnp.int32)
    return flat.reshape(-1, 1), flat.reshape(-1, SLOT)


def dot(a, b):
    return jnp.dot(a, b, preferred_element_type=F32)


def dot_nt(a, b):
    return lax.dot_general(a, b, (((1,), (1,)), ((), ())), preferred_element_type=F32)


def dot_tn(a, b):
    return lax.dot_general(a, b, (((0,), (0,)), ((), ())), preferred_element_type=F32)


def select(idx, source):
    count = source.shape[0]
    lane = lax.broadcasted_iota(jnp.int32, (idx.shape[0], count), 1)
    hot = jnp.where(idx == lane, 1.0, 0.0).astype(BF16)
    return dot(hot, source).astype(BF16)


def norm_parts(x):
    centred = x - jnp.mean(x, axis=-1, keepdims=True)
    inverse = lax.rsqrt(jnp.mean(centred * centred, axis=-1, keepdims=True) + EPSILON)
    return centred * inverse, inverse


def norm_back(hat, inverse, gain, dy):
    grad_gain = jnp.sum(dy * hat, axis=0, keepdims=True)
    t = dy * gain
    dx = inverse * (
        t
        - jnp.mean(t, axis=-1, keepdims=True)
        - hat * jnp.mean(t * hat, axis=-1, keepdims=True)
    )
    return dx.astype(BF16), grad_gain


PACK = LANES // HEAD


def head_masks():
    lane = lax.broadcasted_iota(jnp.int32, (1, LANES), 1) // HEAD
    return [jnp.where(lane == h, 1.0, 0.0).astype(BF16) for h in range(PACK)]


def stack_heads(x, masks):
    return jnp.concatenate([x * m for m in masks], axis=0)


def pick_heads(o):
    lane = lax.broadcasted_iota(jnp.int32, (SLOT, LANES), 1) // HEAD
    out = o[:SLOT]
    for h in range(1, PACK):
        out = jnp.where(lane == h, o[h * SLOT : (h + 1) * SLOT], out)
    return out


def window_bias(lc_ref, lr_ref, w):
    lc = lc_ref[w * SLOT : (w + 1) * SLOT, :]
    lr = lr_ref[w : w + 1, :]
    bias = jnp.where((lc == lr) | (lc < 0), 0.0, MASKED)
    bias = jnp.where(lr < 0, -1e30, bias)
    return jnp.concatenate([bias] * PACK, axis=0)


def soft(qs, k, bias):
    raised = jnp.exp(dot_nt(qs, k) * HEAD ** (-0.5) + bias)
    return raised * (1.0 / jnp.sum(raised, axis=-1, keepdims=True))


def unit_back(qs, k, v, weights, wb, dm, masks):
    dms = stack_heads(dm, masks)
    dw = dot_nt(dms, v).astype(BF16).astype(F32)
    ds = weights * (dw - jnp.sum(dw * weights, axis=-1, keepdims=True))
    ds = (ds * HEAD ** (-0.5)).astype(BF16)
    dq = pick_heads(dot(ds, k))
    dk = dot_tn(ds, qs)
    dv = dot_tn(wb, dms)
    return dq.astype(BF16), dk.astype(BF16), dv.astype(BF16)


def fill_tile(scratch, tile, pitch):
    count, wide, _ = tile.shape
    for r in range(count):
        scratch[r * pitch : r * pitch + wide, :] = tile[r]


def fill_ext(scratch, tile, below, side, corner):
    rows, cols, _ = tile.shape
    pitch = pitch_of(cols)
    scratch[...] = jnp.zeros_like(scratch)
    fill_tile(scratch, tile, pitch)
    base = rows * pitch
    for r in range(MARGIN):
        scratch[base + r * pitch : base + r * pitch + cols, :] = below[r]
    base += MARGIN * pitch
    for r in range(rows):
        scratch[base + r * PM : base + r * PM + MARGIN, :] = side[r]
    for r in range(MARGIN):
        scratch[base + (rows + r) * PM : base + (rows + r) * PM + MARGIN, :] = corner[r]


def put_pieces(idx, source, row_ref, col_ref, corner_ref):
    got = select(idx[...], source)
    a, b = row_ref.shape[0], col_ref.shape[0]
    row_ref[...] = got[:a]
    col_ref[...] = got[a : a + b]
    corner_ref[...] = got[a + b :]


def kernel_one(
    tok, below, side, corner, idx_a, idx_q, idx_p, lc, lr, gain, qkv, proj,
    rolled, packed, mixed, win, quad, p_row, p_col, p_cor, ext,
):
    width = proj.shape[0]
    fill_ext(ext, tok, below, side, corner)
    pitch = pitch_of(tok.shape[1])
    quad[...] = select(idx_q[...], ext[: tok.shape[0] * pitch, :])
    hat, _ = norm_parts(select(idx_a[...], ext[...]).astype(F32))
    normed = (hat * gain[...]).astype(BF16)
    rolled[...] = normed
    packed[...] = dot(normed, qkv[...]).astype(BF16)
    masks = head_masks()
    for w in range(lr.shape[0]):
        bias = window_bias(lc, lr, w)
        at = slice(w * SLOT, (w + 1) * SLOT)
        for g in range(width // LANES):
            lanes = [slice(t * width + g * LANES, t * width + (g + 1) * LANES) for t in range(3)]
            qs = stack_heads(packed[at, lanes[0]], masks)
            wb = soft(qs, packed[at, lanes[1]], bias).astype(BF16)
            mixed[at, lanes[0]] = pick_heads(dot(wb, packed[at, lanes[2]])).astype(BF16)
    out = dot(mixed[...], proj[...]).astype(BF16)
    win[...] = out
    put_pieces(idx_p, out, p_row, p_col, p_cor)


def kernel_two(win, below, side, corner, idx, quad, gain_m, weight, gain_3, section, merged, normed3):
    ext = jnp.concatenate([win[...], below[...], side[...], corner[...]], axis=0)
    restored = select(idx[...], ext)
    total = (quad[...].astype(F32) + restored.astype(F32)).astype(BF16)
    section[...] = total
    t3 = merged.shape[0]
    joined = jnp.concatenate([total[k * t3 : (k + 1) * t3] for k in range(4)], axis=1)
    hat, _ = norm_parts(joined.astype(F32))
    out = dot((hat * gain_m[...]).astype(BF16), weight[...]).astype(BF16)
    merged[...] = out
    hat3, _ = norm_parts(out.astype(F32))
    normed3[...] = (hat3 * gain_3[...]).astype(BF16)


def kernel_three(
    tile, below, side, corner, cot, c_below, c_side, c_corner, idx_a, idx_p, lc, lr, qkv, proj,
    both, p_row, p_col, p_cor, grads, ext, packed, mixed, dpacked,
):
    width = proj.shape[0]
    fill_ext(ext, cot, c_below, c_side, c_corner)
    idx = idx_a[...]
    dproj = select(idx, ext[...])
    rolled = select(
        idx, jnp.concatenate([tile[...], below[...], side[...], corner[...]], axis=0)
    )
    packed[...] = dot(rolled, qkv[...]).astype(BF16)
    dmixed = dot_nt(dproj, proj[...]).astype(BF16)
    masks = head_masks()
    for w in range(lr.shape[0]):
        bias = window_bias(lc, lr, w)
        at = slice(w * SLOT, (w + 1) * SLOT)
        for g in range(width // LANES):
            lanes = [slice(t * width + g * LANES, t * width + (g + 1) * LANES) for t in range(3)]
            qs = stack_heads(packed[at, lanes[0]], masks)
            k, v = packed[at, lanes[1]], packed[at, lanes[2]]
            weights = soft(qs, k, bias)
            wb = weights.astype(BF16)
            mixed[at, lanes[0]] = pick_heads(dot(wb, v)).astype(BF16)
            back = unit_back(qs, k, v, weights, wb, dmixed[at, lanes[0]], masks)
            for t in range(3):
                dpacked[at, lanes[t]] = back[t]
    both[:, :width] = dot(mixed[...], proj[...]).astype(BF16)
    both[:, width:] = dot_nt(dpacked[...], qkv[...]).astype(BF16)
    put_pieces(idx_p, both[...], p_row, p_col, p_cor)
    grads[:, : 3 * width] = dot_tn(rolled, dpacked[...]).astype(BF16)
    grads[:, 3 * width :] = dot_tn(mixed[...], dproj).astype(BF16)


def kernel_four(
    both, below, side, corner, idx, idx_p, cot, merged, section, gain_m, gain_3, weight,
    out, dsec, p_row, p_col, p_cor, grad, g_m, g_3, cots,
):
    width = merged.shape[1]
    rows, cols, _ = cot.shape
    pitch = pitch_of(cols)
    cots[...] = jnp.zeros_like(cots)
    fill_tile(cots, cot, pitch)
    ext = jnp.concatenate([both[...], below[...], side[...], corner[...]], axis=0)
    back = select(idx[...], ext)
    mine = merged[...].astype(F32)
    total = (mine + back[:, :width].astype(F32)).astype(BF16)
    for r in range(rows):
        out[r] = total[r * pitch : r * pitch + cols]
    hat3, inv3 = norm_parts(mine)
    dmerged, grad3 = norm_back(hat3, inv3, gain_3[...], back[:, width:].astype(F32))
    g_3[...] = grad3
    dmerged = cots[...] + dmerged
    t3 = merged.shape[0]
    joined = jnp.concatenate([section[k * t3 : (k + 1) * t3, :] for k in range(4)], axis=1)
    hat, inv = norm_parts(joined.astype(F32))
    normed = (hat * gain_m[...]).astype(BF16)
    djn = dot_nt(dmerged, weight[...]).astype(BF16).astype(F32)
    djoined, gradm = norm_back(hat, inv, gain_m[...], djn)
    g_m[...] = gradm
    narrow = dsec.shape[1]
    ds = jnp.concatenate([djoined[:, k * narrow : (k + 1) * narrow] for k in range(4)], axis=0)
    dsec[...] = ds
    put_pieces(idx_p, ds, p_row, p_col, p_cor)
    grad[...] = dot_tn(normed, dmerged).astype(BF16)


def kernel_five(
    dsec, below, side, corner, idx_a, idx_p, lc, lr, packed, rolled, mixed, qkv, proj,
    drolled, p_row, p_col, p_cor, grads, dpacked,
):
    width = proj.shape[0]
    ext = jnp.concatenate([dsec[...], below[...], side[...], corner[...]], axis=0)
    dproj = select(idx_a[...], ext)
    dmixed = dot_nt(dproj, proj[...]).astype(BF16)
    masks = head_masks()
    for w in range(lr.shape[0]):
        bias = window_bias(lc, lr, w)
        at = slice(w * SLOT, (w + 1) * SLOT)
        for g in range(width // LANES):
            lanes = [slice(t * width + g * LANES, t * width + (g + 1) * LANES) for t in range(3)]
            qs = stack_heads(packed[at, lanes[0]], masks)
            k, v = packed[at, lanes[1]], packed[at, lanes[2]]
            weights = soft(qs, k, bias)
            back = unit_back(
                qs, k, v, weights, weights.astype(BF16), dmixed[at, lanes[0]], masks
            )
            for t in range(3):
                dpacked[at, lanes[t]] = back[t]
    out = dot_nt(dpacked[...], qkv[...]).astype(BF16)
    drolled[...] = out
    put_pieces(idx_p, out, p_row, p_col, p_cor)
    grads[:, : 3 * width] = dot_tn(rolled[...], dpacked[...]).astype(BF16)
    grads[:, 3 * width :] = dot_tn(mixed[...], dproj).astype(BF16)


def kernel_six(win, below, side, corner, idx, idx_n, tok, dsec, gain, out, g_2, toks):
    rows, cols, _ = tok.shape
    pitch = pitch_of(cols)
    toks[...] = jnp.zeros_like(toks)
    fill_tile(toks, tok, pitch)
    ext = jnp.concatenate([win[...], below[...], side[...], corner[...]], axis=0)
    dnormed = select(idx[...], ext).astype(F32)
    hat, inv = norm_parts(toks[...].astype(F32))
    dtok, grad = norm_back(hat, inv, gain[...], dnormed)
    g_2[...] = grad
    total = select(idx_n[...], dsec[...]) + dtok
    for r in range(rows):
        out[r] = total[r * pitch : r * pitch + cols]


def call(kernel, outs, scratch, name, args, cost=12e6):
    return pl.pallas_call(
        kernel,
        out_shape=[jax.ShapeDtypeStruct(s, d) for s, d in outs],
        scratch_shapes=[pltpu.VMEM(s, BF16) for s in scratch],
        cost_estimate=pl.CostEstimate(flops=10**9, bytes_accessed=int(cost), transcendentals=0),
        name=name,
    )(*args)


def passed_along(value, axis, by):
    count = lax.axis_size(axis)
    return lax.ppermute(value, axis, [(i, (i + by) % count) for i in range(count)])


def passed_diagonal(value, by):
    nr, nc = lax.axis_size("rows"), lax.axis_size("cols")
    pairs = [
        (r * nc + c, ((r + by) % nr) * nc + (c + by) % nc) for r in range(nr) for c in range(nc)
    ]
    return lax.ppermute(value, ("rows", "cols"), pairs)


def exchange(pieces, by):
    row, col, corner = pieces
    return (
        passed_along(row, "rows", by),
        passed_along(col, "cols", by),
        passed_diagonal(corner, by),
    )


def add_up(terms):
    total = terms[0].astype(F32)
    for term in terms[1:]:
        total = total + term.astype(F32)
    return total


def scatter_sum(grads):
    nr, nc = lax.axis_size("rows"), lax.axis_size("cols")
    chips = nc // 2
    me = lax.axis_index("cols")
    core, chip, row = me % 2, me // 2, lax.axis_index("rows")
    depth, width = grads.shape
    parts = grads.reshape(nr, chips, 2, depth // (nr * nc), width)
    keep = lax.dynamic_index_in_dim(parts, core, 2, keepdims=False)
    send = lax.dynamic_index_in_dim(parts, 1 - core, 2, keepdims=False)
    got = lax.ppermute(send, "cols", [(i, i ^ 1) for i in range(nc)])
    half = add_up([keep, got]).astype(BF16)
    terms = [lax.dynamic_index_in_dim(half, chip, 1, keepdims=False)]
    for d in range(1, chips):
        send = lax.dynamic_index_in_dim(half, (chip + d) % chips, 1, keepdims=False)
        pairs = [(i, (i + 2 * d) % nc) for i in range(nc)]
        terms.append(lax.ppermute(send, "cols", pairs))
    part = add_up(terms).astype(BF16)
    terms = [lax.dynamic_index_in_dim(part, row, 0, keepdims=False)]
    for d in range(1, nr):
        send = lax.dynamic_index_in_dim(part, (row + d) % nr, 0, keepdims=False)
        terms.append(passed_along(send, "rows", d))
    return add_up(terms).astype(BF16)


def sum_all(value):
    nr, nc = lax.axis_size("rows"), lax.axis_size("cols")
    value = value + lax.ppermute(value, "cols", [(i, i ^ 1) for i in range(nc)])
    total = value
    for d in range(1, nc // 2):
        total = total + lax.ppermute(value, "cols", [(i, (i + 2 * d) % nc) for i in range(nc)])
    value = total
    for d in range(1, nr):
        total = total + passed_along(value, "rows", d)
    return total


def on_device(
    tokens, cotangent, shifts, norm2_gain, qkv2, proj2, merge_gain, merge_weight, norm3_gain,
    qkv3, proj3,
):
    rows, cols, narrow = tokens.shape
    wide = qkv3.shape[0]
    rows3, cols3 = rows // 2, cols // 2
    pitch, pitch3 = pitch_of(cols), pitch_of(cols3)
    base, base3 = rows * pitch, rows3 * pitch3
    r, c = lax.axis_index("rows"), lax.axis_index("cols")
    s0, s1, s2, s3 = shifts[0], shifts[1], shifts[2], shifts[3]

    win2, win3 = window_tokens(rows, cols), window_tokens(rows3, cols3)
    n2, n3 = len(win2[0]), len(win3[0])
    quad = quad_tokens(rows, cols)
    nat = grid_tokens(rows, cols, pitch)
    grid3 = grid_tokens(rows3, cols3, pitch3)
    as_grid = lambda h, w: h * pitch + w
    as_grid3 = lambda h, w: h * pitch3 + w
    as_quad = lambda h, w: quad_index(h, w, rows, cols)
    as_win = lambda h, w: win_index(h, w, cols)
    as_win3 = lambda h, w: win_index(h, w, cols3)
    fixed = lambda t, inner: np.where(t[2], inner(t[0], t[1]), -1).astype(np.int32).reshape(-1, 1)

    idx_a = ahead_index(*win2, s0, s1, rows, cols, as_grid, base)
    idx_h = ahead_index(*win2, s0, s1, rows, cols, as_quad, len(quad[0]))
    idx_d = ahead_index(*win3, s2, s3, rows3, cols3, as_grid3, base3)
    idx_c = behind_index(*quad, s0, s1, rows, cols, n2)
    idx_i = behind_index(*nat, s0, s1, rows, cols, n2)
    idx_f = behind_index(*grid3, s2, s3, rows3, cols3, n3)
    idx_q = fixed(quad, as_grid)
    idx_n = fixed(nat, as_quad)
    idx_b = piece_index(rows, cols, as_win, False)
    idx_e = piece_index(rows3, cols3, as_win3, False)
    idx_g = piece_index(rows, cols, as_quad, True)
    lc2, lr2 = window_labels(rows, cols, r, c, s0, s1)
    lc3, lr3 = window_labels(rows3, cols3, r, c, s2, s3)
    gain2, gainm, gain3 = (g.reshape(1, -1) for g in (norm2_gain, merge_gain, norm3_gain))

    def first(x):
        return x[:MARGIN], x[:, :MARGIN], x[:MARGIN, :MARGIN]

    sizes = piece_sizes(rows, cols)
    sizes3 = piece_sizes(rows3, cols3)
    ext = base + MARGIN * pitch + (rows + MARGIN) * PM
    ext3 = base3 + MARGIN * pitch3 + (rows3 + MARGIN) * PM
    quads = len(quad[0])

    tok_halo = exchange(first(tokens), -1)
    cot_halo = exchange(first(cotangent), -1)

    rolled, packed, mixed, win, tquad, *pieces = call(
        kernel_one,
        [((n2, narrow), BF16), ((n2, 3 * narrow), BF16), ((n2, narrow), BF16),
         ((n2, narrow), BF16), ((quads, narrow), BF16)]
        + [((s, narrow), BF16) for s in sizes],
        [(ext, narrow)],
        "section_two",
        (tokens, *tok_halo, idx_a, idx_q, idx_b, lc2, lr2, gain2, qkv2, proj2),
    )
    halo = exchange(pieces, 1)
    section, merged, normed3 = call(
        kernel_two,
        [((quads, narrow), BF16), ((base3, wide), BF16), ((base3, wide), BF16)],
        [],
        "merge",
        (win, *halo, idx_c, tquad, gainm, merge_weight, gain3),
    )
    if PM == pitch3:
        side3 = normed3
    else:
        side3 = normed3.reshape(rows3, pitch3, wide)[:, :PM].reshape(rows3 * PM, wide)
    corner3 = side3[: MARGIN * PM]
    halo = exchange((normed3[: MARGIN * pitch3], side3, corner3), -1)
    both, p_row, p_col, p_cor, grads3 = call(
        kernel_three,
        [((n3, 2 * wide), BF16)]
        + [((s, 2 * wide), BF16) for s in sizes3]
        + [((wide, 4 * wide), BF16)],
        [(ext3, wide), (n3, 3 * wide), (n3, wide), (n3, 3 * wide)],
        "section_three",
        (normed3, *halo, cotangent, *cot_halo, idx_d, idx_e, lc3, lr3, qkv3, proj3),
    )
    halo = exchange((p_row, p_col, p_cor), 1)
    out, dsec, p_row, p_col, p_cor, grads_m, g_m, g_3 = call(
        kernel_four,
        [(cotangent.shape, BF16), ((quads, narrow), BF16)]
        + [((s, narrow), BF16) for s in sizes]
        + [((4 * narrow, wide), BF16), ((1, 4 * narrow), F32), ((1, wide), F32)],
        [(base3, wide)],
        "merge_back",
        (both, *halo, idx_f, idx_g, cotangent, merged, section, gainm, gain3, merge_weight),
    )
    halo = exchange((p_row, p_col, p_cor), -1)
    drolled, p_row, p_col, p_cor, grads2 = call(
        kernel_five,
        [((n2, narrow), BF16)]
        + [((s, narrow), BF16) for s in sizes]
        + [((narrow, 4 * narrow), BF16)],
        [(n2, 3 * narrow)],
        "section_two_back",
        (dsec, *halo, idx_h, idx_b, lc2, lr2, packed, rolled, mixed, qkv2, proj2),
    )
    halo = exchange((p_row, p_col, p_cor), 1)
    tokens_grad, g_2 = call(
        kernel_six,
        [(tokens.shape, BF16), ((1, narrow), F32)],
        [(base, narrow)],
        "tokens_back",
        (drolled, *halo, idx_i, idx_n, tokens, dsec, gain2),
    )
    sum3, sum_m, sum2 = scatter_sum(grads3), scatter_sum(grads_m), scatter_sum(grads2)
    gains = sum_all(jnp.concatenate([g_2, g_m, g_3], axis=1)).reshape(-1)
    return (
        out,
        tokens_grad,
        gains,
        sum2[:, : 3 * narrow].reshape(-1),
        sum2[:, 3 * narrow :].reshape(-1),
        sum_m.reshape(-1),
        sum3[:, : 3 * wide].reshape(-1),
        sum3[:, 3 * wide :].reshape(-1),
    )


def solution(mesh):
    tile = P(("groups", "rows"), "cols", None)
    spread = P(("groups", "rows", "cols"))
    return jax.shard_map(
        on_device,
        mesh=mesh,
        in_specs=(tile, tile) + (P(),) * 9,
        out_specs=(tile, tile, P("groups")) + (spread,) * 5,
        check_vma=False,
    )
```

time: 388 us -> 157 us (0.40)
  blocking collectives: 162 us -> 0 us
  local copies, waits for them, and re-layouts: 98.1 us -> 26.8 us
  matrix products: 41.8 us -> 0 us
  Pallas kernels: 0 us -> 34.8 us
  waiting for transfers between devices: 11.3 us -> 44.4 us
  other arithmetic: 32.8 us -> 9.71 us
  starting transfers between devices: 17.1 us -> 37.1 us
  between operations: 20.6 us -> 3.71 us
    psum x1 -> x0, blocking collectives: 162 us -> none  [on_device(): lax.psum(jnp.concatenate([grad_gain_two, grad_gain_merge, grad_gain_three...]
    dot_general x27 -> x0, matrix products: 41.8 us -> none  [the longest x6 9.14 us: attend(): jnp.einsum('nphd,nqhd->nhpq', queries, key_part) * head_size ** (-0.5)]
    pallas_call x0 -> x6, Pallas kernels: none -> 34.8 us  [call(): pl.pallas_call(kernel, out_shape=[jax.ShapeDtypeStruct(s, d) for s, d in...]
    convert_element_type x18 -> x0, local copies, waits for them, and re-layouts: 23 us -> none  [the longest x4 6.49 us: normalize(): widened = inputs.astype(jnp.float32)]
    ppermute x0 -> x15, waiting for transfers between devices: none -> 22.4 us  [the longest x7 10.9 us: passed_diagonal(): return lax.ppermute(value, ('rows', 'cols'), pairs)]
    slice x32 -> x10, local copies, waits for them, and re-layouts: 22.4 us -> 7.36 us  [the longest x6 4.99 us: first(): return (x[:MARGIN], x[:, :MARGIN], x[:MARGIN, :MARGIN])]
    reduce_sum x11 -> x0, other arithmetic: 11.8 us -> none  [the longest x5 6.71 us: normalize(): return (centred * lax.rsqrt(spread + EPSILON) * gain).astype(jnp.bfloat16)]
    ppermute x16 -> x26, waiting for transfers between devices: 11.3 us -> 21.9 us  [passed_along(): lax.ppermute(value, axis, [(i, (i + by) % count) for i in range(count)])]
  transfers between devices with their start and end apart: 16 -> 41, of which waited for: 6 -> 15; matrix products, arithmetic and copies ran while one was open for 20% -> 18% of each run, Pallas kernels for 0% -> 7%
where the time goes in v1:
time: 157 us; the launch traced here: 156 us
  waiting for transfers between devices  44.4 us (28%)
  starting transfers between devices  37.1 us (24%)
  Pallas kernels  34.8 us (22%)
  local copies, waits for them, and re-layouts  26.8 us (17%)
  other arithmetic  9.71 us (6%)
  between operations  3.71 us (2%)
    pallas_call x6, Pallas kernels, call(): pl.pallas_call(kernel, out_shape=[jax.ShapeDtypeStruct(s, d) for s, d in...  34.8 us
    ppermute x26, starting transfers between devices, passed_along(): lax.ppermute(value, axis, [(i, (i + by) % count) for i in range(count)])  26.5 us
    ppermute x26, waiting for transfers between devices, passed_along(): lax.ppermute(value, axis, [(i, (i + by) % count) for i in range(count)])  21.9 us
    ppermute x7, waiting for transfers between devices, passed_diagonal(): return lax.ppermute(value, ('rows', 'cols'), pairs)  10.9 us
    unnamed x83, local copies, waits for them, and re-layouts  7.96 us
    ppermute x3, waiting for transfers between devices, scatter_sum(): terms.append(lax.ppermute(send, 'cols', pairs))  7.53 us
    ppermute x7, starting transfers between devices, passed_diagonal(): return lax.ppermute(value, ('rows', 'cols'), pairs)  6.81 us
    slice x6, local copies, waits for them, and re-layouts, first(): return (x[:MARGIN], x[:, :MARGIN], x[:MARGIN, :MARGIN])  4.99 us
  transfers between devices with their start and end apart: 41, of which 15 were waited for; matrix products, arithmetic and copies ran while one was open for 18% of the time, Pallas kernels for 7%

profile of v1, /device:TPU:0, one launch (start us, length us, event | category | flops | bytes accessed | tf_op | source)
XLA Modules:
  0.0 156.5 jit_solution(18070177744830427501)
XLA Ops:
  0.6 0.9 slice.46
  1.5 5.1 %collective-permute-start = (bf16[6,28,256]{2,1,0:T(8,128)(2,1)S(1)}, bf16[6,28,256]{2,1,0:T(8,128)(2,1)S(1)}, u32[]{:S(2)}, u32[]{:S(2)}) collective-permute-start(bf16[6,28,256]{2,1,0:T(8,128)(2,1)S(1)} %slice.46), channel_id=1, source_target_pairs={{0,12},{4,0},{8,4},{12,8},{1,13},{5,1},{9,5},{13,9},{2,14},{6,2},{... | collective-permute-start | bytes 258056 | tf_op jit(solution)/shard_map/ppermute | solution.py:385
  9.7 0.9 slice.52
  11.8 1.4 fusion.127
  14.5 2.0 %fusion.65 = (s32[512]{0:T(512)S(1)}, s32[512]{0:T(512)S(1)}, s32[512]{0:T(512)S(1)}) fusion(pred[512]{0:T(512)(128)(4,1)} %constant.347.clone, s32[512]{0:T(512)} %constant.346.clone, s32[512]{0:T(512)} %constant.345.clone, s32[]{:T(128)} %bitcast.1, s32[]{:T(128)} %bitcast, s32[]{:T(128)S(6)} %sub.110, s32[]{:T(128)S(6)} %mul.114, s32[]{:T(128)S(6)} %sub.109, ...), kind=kLoop, calls=%fused_computation.142 | loop fusion | flops 40448 | bytes 10776 | tf_op jit(solution)/shard_map/jit(_where)/select_n | solution.py:69
  16.6 0.9 copy.48.idx_a
  18.1 0.9 copy.49.lc
  19.7 5.0 %section_two.1 = (bf16[512,256]{1,0:T(8,128)(2,1)}, bf16[512,768]{1,0:T(8,128)(2,1)}, bf16[512,256]{1,0:T(8,128)(2,1)}, bf16[512,256]{1,0:T(8,128)(2,1)}, bf16[4...) custom-call(bf16[14,28,256]{2,1,0:T(8,128)(2,1)} %tok.3, ...), custom_call_target="tpu_custom_call" | custom-call | flops 1000000000 | bytes 12000000 | tf_op jit(solution)/shard_map/section_two/pallas_call | solution.py:374
  24.7 1.6 %collective-permute-start.3 = (bf16[192,256]{1,0:T(8,128)(2,1)}, bf16[192,256]{1,0:T(8,128)(2,1)S(1)}, u32[]{:S(2)}, u32[]{:S(2)}) collective-permute-start(bf16[192,256]{1,0:T(8,128)(2,1)} %get-tuple-element.40), channel_id=1, source_target_pairs={{0,4},{4,8},{8,12},{12,0},{1,5},{5,9},{9,13},{13,1},{2,6},{6,10},{... | collective-permute-start | bytes 294920 | tf_op jit(solution)/shard_map/ppermute | solution.py:385
  26.5 2.1 %collective-permute-start.5 = (bf16[96,256]{1,0:T(8,128)(2,1)}, bf16[96,256]{1,0:T(8,128)(2,1)S(1)}, u32[]{:S(2)}, u32[]{:S(2)}) collective-permute-start(bf16[96,256]{1,0:T(8,128)(2,1)} %get-tuple-element.42), channel_id=1, source_target_pairs={{0,5},{1,6},{2,7},{3,4},{4,9},{5,10},{6,11},{7,8},{8,13},{9,14},{1... | collective-permute-start | bytes 147464 | tf_op jit(solution)/shard_map/ppermute | solution.py:393
  28.7 1.3 fusion.94
  32.9 2.3 %collective-permute-start.11 = (bf16[6,6,512]{2,1,0:T(8,128)(2,1)S(1)}, bf16[6,6,512]{2,1,0:T(8,128)(2,1)S(1)}, u32[]{:S(2)}, u32[]{:S(2)}) collective-permute-start(bf16[6,6,512]{2,1,0:T(8,128)(2,1)S(1)} %slice.54), channel_id=1, source_target_pairs={{0,15},{1,12},{2,13},{3,14},{4,3},{5,0},{6,1},{7,2},{8,7},{9,4},{1... | collective-permute-start | bytes 110600 | tf_op jit(solution)/shard_map/ppermute | solution.py:393
  36.0 3.6 %merge.1 = (bf16[448,256]{1,0:T(8,128)(2,1)}, bf16[112,512]{1,0:T(8,128)(2,1)}, bf16[112,512]{1,0:T(8,128)(2,1)}) custom-call(bf16[512,256]{1,0:T(8,128)(2,1)} %get-tuple-element.39.win, bf16[192,256]{1,0:T(8,128)(2,1)} %copy-done.28, bf16[224,256]{1,0:T(8,128)(2,1)} %copy-done.22, bf16[96,256]{1,0:T(8,128)(2,1)} %copy-done.35, s32[448,1]{1,0:T(8,128)} %copy.50.idx, ...), custom_call_target="tpu_custom_call" | custom-call | flops 1000000000 | bytes 12000000 | tf_op jit(solution)/shard_map/merge/pallas_call | solution.py:374
  39.6 0.9 slice.51
  41.9 1.3 fusion.121
  45.3 1.5 collective-permute-done.6.below
  48.1 8.5 %section_three.1 = (bf16[128,1024]{1,0:T(8,128)(2,1)}, bf16[96,1024]{1,0:T(8,128)(2,1)}, bf16[112,1024]{1,0:T(8,128)(2,1)}, bf16[96,1024]{1,0:T(8,128)(2,1)}, bf16[512,2048]{1,0:T(8,128)(2,1)}) custom-call(bf16[112,512]{1,0:T(8,128)(2,1)} %get-tuple-element.44.tile, bf16[96,512]{1,0:T(8,128)(2,1)} %copy-done.27, bf16[112,512]{1,0:T(8,128)(2,1)} %copy-done.21, ...), custom_call_target="tpu_custom_call" | custom-call | flops 1000000000 | bytes 12000000 | tf_op jit(solution)/shard_map/section_three/pallas_call | solution.py:374
  56.6 1.2 collective-permute-start.13
  58.6 1.3 select_bitcast_fusion
  60.7 7.0 %collective-permute-done.12.below = bf16[96,1024]{1,0:T(8,128)(2,1)S(1)} collective-permute-done((bf16[96,1024]{1,0:T(8,128)(2,1)}, bf16[96,1024]{1,0:T(8,128)(2,1)S(1)}, u32[]{:S(2)}, u32[]{:S(2)}) %collective-permute-start.12) | collective-permute-done | bytes 196640 | tf_op jit(solution)/shard_map/ppermute | solution.py:385
  67.6 2.9 %collective-permute-done.14.corner = bf16[96,1024]{1,0:T(8,128)(2,1)S(1)} collective-permute-done((bf16[96,1024]{1,0:T(8,128)(2,1)}, bf16[96,1024]{1,0:T(8,128)(2,1)S(1)}, u32[]{:S(2)}, u32[]{:S(2)}) %collective-permute-start.14) | collective-permute-done | bytes 196640 | tf_op jit(solution)/shard_map/ppermute | solution.py:393
  71.2 4.4 %merge_back.1 = (bf16[7,14,512]{2,1,0:T(8,128)(2,1)}, bf16[448,256]{1,0:T(8,128)(2,1)}, bf16[192,256]{1,0:T(8,128)(2,1)}, bf16[224,256]{1,0:T(8,128)(2,1)}, bf16...) custom-call(bf16[128,1024]{1,0:T(8,128)(2,1)} %get-tuple-element.45.both, ...), custom_call_target="tpu_custom_call" | custom-call | flops 1000000000 | bytes 12000000 | tf_op jit(solution)/shard_map/merge_back/pallas_call | solution.py:374
  75.6 0.9 collective-permute-start.16
  77.1 0.9 copy.54.idx_a
  78.8 2.3 %collective-permute-done.17.corner = bf16[96,256]{1,0:T(8,128)(2,1)S(1)} collective-permute-done((bf16[96,256]{1,0:T(8,128)(2,1)}, bf16[96,256]{1,0:T(8,128)(2,1)S(1)}, u32[]{:S(2)}, u32[]{:S(2)}) %collective-permute-start.17) | collective-permute-done | bytes 49184 | tf_op jit(solution)/shard_map/ppermute | solution.py:393
  82.4 10.2 %section_two_back.1 = (bf16[512,256]{1,0:T(8,128)(2,1)}, bf16[192,256]{1,0:T(8,128)(2,1)}, bf16[224,256]{1,0:T(8,128)(2,1)}, bf16[96,256]{1,0:T(8,128)(2,1)}, bf16[256,1024]{1,0:T(8,128)(2,1)}) custom-call(bf16[448,256]{1,0:T(8,128)(2,1)} %get-tuple-element.52.dsec, bf16[192,256]{1,0:T(8,128)(2,1)} %copy-done.26, bf16[224,256]{1,0:T(8,128)(2,1)} %copy-done.20, ...), custom_call_target="tpu_custom_call" | custom-call | flops 1000000000 | bytes 12000000 | tf_op jit(solution)/shard_map/section_two_back/pallas_call | solution.py:374
  92.7 1.0 collective-permute-start.18
  94.5 1.1 dynamic-slice_bitcast_fusion.4
  96.0 5.7 %collective-permute-done.20.corner = bf16[96,256]{1,0:T(8,128)(2,1)S(1)} collective-permute-done((bf16[96,256]{1,0:T(8,128)(2,1)}, bf16[96,256]{1,0:T(8,128)(2,1)S(1)}, u32[]{:S(2)}, u32[]{:S(2)}) %collective-permute-start.20) | collective-permute-done | bytes 49184 | tf_op jit(solution)/shard_map/ppermute | solution.py:393
  103.0 3.0 %tokens_back.1 = (bf16[14,28,256]{2,1,0:T(8,128)(2,1)}, f32[1,256]{1,0:T(1,128)}) custom-call(bf16[512,256]{1,0:T(8,128)(2,1)} %get-tuple-element.59.win, bf16[192,256]{1,0:T(8,128)(2,1)} %copy-done.30, bf16[224,256]{1,0:T(8,128)(2,1)} %copy-done.23, bf16[96,256]{1,0:T(8,128)(2,1)} %copy-done.36, s32[448,1]{1,0:T(8,128)} %copy.56.idx, ...), custom_call_target="tpu_custom_call" | custom-call | flops 1000000000 | bytes 12000000 | tf_op jit(solution)/shard_map/tokens_back/pallas_call | solution.py:374
  106.8 1.1 collective-permute-done.21
  108.7 2.9 %collective-permute-done.22 = f32[1,1792]{1,0:T(1,128)S(1)} collective-permute-done((f32[1,1792]{1,0:T(1,128)S(1)}, f32[1,1792]{1,0:T(1,128)S(1)}, u32[]{:S(2)}, u32[]{:S(2)}) %collective-permute-start.22) | collective-permute-done | bytes 7200 | tf_op jit(solution)/shard_map/ppermute | solution.py:441
  111.8 1.9 %collective-permute-start.23 = (f32[1,1792]{1,0:T(1,128)S(1)}, f32[1,1792]{1,0:T(1,128)S(1)}, u32[]{:S(2)}, u32[]{:S(2)}) collective-permute-start(f32[1,1792]{1,0:T(1,128)S(1)} %add.499), channel_id=1, source_target_pairs={{0,4},{4,8},{8,12},{12,0},{1,5},{5,9},{9,13},{13,1},{2,6},{6,10},{... | collective-permute-start | bytes 21512 | tf_op jit(solution)/shard_map/ppermute | solution.py:385
  113.7 1.1 fusion.4
  115.5 1.0 dynamic-slice_bitcast_fusion
  116.5 1.2 collective-permute-done.23
  118.4 1.5 collective-permute-done.27
  119.9 2.4 %collective-permute-start.30 = (bf16[16,1024]{1,0:T(8,128)(2,1)S(1)}, bf16[16,1024]{1,0:T(8,128)(2,1)S(1)}, u32[]{:S(2)}, u32[]{:S(2)}) collective-permute-start(bf16[16,1024]{1,0:T(8,128)(2,1)S(1)} %get-tuple-element.77), channel_id=1, source_target_pairs={{0,12},{4,0},{8,4},{12,8},{1,13},{5,1},{9,5},{13,9},{2,14},{6,2},{... | collective-permute-start | bytes 98312 | tf_op jit(solution)/shard_map/ppermute | solution.py:385
  123.0 1.9 %collective-permute-start.28 = (bf16[16,1024]{1,0:T(8,128)(2,1)S(1)}, bf16[16,1024]{1,0:T(8,128)(2,1)S(1)}, u32[]{:S(2)}, u32[]{:S(2)}) collective-permute-start(bf16[16,1024]{1,0:T(8,128)(2,1)S(1)} %get-tuple-element.76), channel_id=1, source_target_pairs={{0,4},{4,8},{8,12},{12,0},{1,5},{5,9},{9,13},{13,1},{2,6},{6,10},{... | collective-permute-start | bytes 98312 | tf_op jit(solution)/shard_map/ppermute | solution.py:385
  125.8 1.4 collective-permute-done.29
  127.2 1.5 collective-permute-done.28
  129.4 1.6 %fusion = bf16[4,2,32,2048]{3,2,1,0:T(8,128)(2,1)S(1)} fusion(bf16[4,2,32,2048]{3,2,1,0:T(8,128)(2,1)} %collective-permute-done.36, bf16[4,2,2,32,2048]{4,3,2,1,0:T(8,128)(2,1)S(1)} %bitcast.87, s32[]{:T(128)S(6)} %select_n.318), kind=kLoop, calls=%fused_computation.1 | loop fusion | flops 2097152 | bytes 3145732 | tf_op jit(solution)/shard_map/convert_element_type | solution.py:422
  131.1 1.3 collective-permute-start.37
  133.1 3.0 %collective-permute-start.35 = (bf16[64,512]{1,0:T(8,128)(2,1)S(1)}, bf16[64,512]{1,0:T(8,128)(2,1)S(1)}, u32[]{:S(2)}, u32[]{:S(2)}) collective-permute-start(bf16[64,512]{1,0:T(8,128)(2,1)S(1)} %get-tuple-element.74), channel_id=1, source_target_pairs={{0,12},{4,0},{8,4},{12,8},{1,13},{5,1},{9,5},{13,9},{2,14},{6,2},{... | collective-permute-start | bytes 196616 | tf_op jit(solution)/shard_map/ppermute | solution.py:385
  136.8 6.0 %collective-permute-done.37 = bf16[4,32,2048]{2,1,0:T(8,128)(2,1)S(1)} collective-permute-done((bf16[4,32,2048]{2,1,0:T(8,128)(2,1)S(1)}, bf16[4,32,2048]{2,1,0:T(8,128)(2,1)S(1)}, u32[]{:S(2)}, u32[]{:S(2)}) %collective-permute-start.37) | collective-permute-done | bytes 524320 | tf_op jit(solution)/shard_map/ppermute | solution.py:427
  143.0 1.9 %collective-permute-start.40 = (bf16[32,2048]{1,0:T(8,128)(2,1)S(1)}, bf16[32,2048]{1,0:T(8,128)(2,1)S(1)}, u32[]{:S(2)}, u32[]{:S(2)}) collective-permute-start(bf16[32,2048]{1,0:T(8,128)(2,1)S(1)} %get-tuple-element.71), channel_id=1, source_target_pairs={{0,12},{4,0},{8,4},{12,8},{1,13},{5,1},{9,5},{13,9},{2,14},{6,2},{... | collective-permute-start | bytes 393224 | tf_op jit(solution)/shard_map/ppermute | solution.py:385
  146.3 4.0 %collective-permute-done.40 = bf16[32,2048]{1,0:T(8,128)(2,1)S(1)} collective-permute-done((bf16[32,2048]{1,0:T(8,128)(2,1)S(1)}, bf16[32,2048]{1,0:T(8,128)(2,1)S(1)}, u32[]{:S(2)}, u32[]{:S(2)}) %collective-permute-start.40) | collective-permute-done | bytes 131104 | tf_op jit(solution)/shard_map/ppermute | solution.py:385
  150.3 4.7 %collective-permute-done.39 = bf16[32,2048]{1,0:T(8,128)(2,1)S(1)} collective-permute-done((bf16[32,2048]{1,0:T(8,128)(2,1)S(1)}, bf16[32,2048]{1,0:T(8,128)(2,1)S(1)}, u32[]{:S(2)}, u32[]{:S(2)}) %collective-permute-start.39) | collective-permute-done | bytes 131104 | tf_op jit(solution)/shard_map/ppermute | solution.py:385
  (171 shorter events, 30.2 us)
Async XLA Ops:
  1.5 17.5 %collective-permute-start = (bf16[6,28,256]{2,1,0:T(8,128)(2,1)S(1)}, bf16[6,28,256]{2,1,0:T(8,128)(2,1)S(1)}, u32[]{:S(2)}, u32[]{:S(2)}) collective-permute-start(bf16[6,28,256]{2,1,0:T(8,128)(2,1)S(1)} %slice.46), channel_id=1, source_target_pairs={{0,12},{4,0},{8,4},{12,8},{1,13},{5,1},{9,5},{13,9},{2,14},{6,2},{... | collective-permute-start | bytes 258056 | tf_op jit(solution)/shard_map/ppermute | solution.py:385
  7.4 11.6 %collective-permute-start.1 = (bf16[14,6,256]{2,1,0:T(8,128)(2,1)S(1)}, bf16[14,6,256]{2,1,0:T(8,128)(2,1)S(1)}, u32[]{:S(2)}, u32[]{:S(2)}) collective-permute-start(bf16[14,6,256]{2,1,0:T(8,128)(2,1)S(1)} %slice.47), channel_id=1, source_target_pairs={{0,3},{1,0},{2,1},{3,2},{4,7},{5,4},{6,5},{7,6},{8,11},{9,8},{10,9... | collective-permute-start | bytes 129032 | tf_op jit(solution)/shard_map/ppermute | solution.py:385
  8.8 10.2 %collective-permute-start.2 = (bf16[6,6,256]{2,1,0:T(8,128)(2,1)S(1)}, bf16[6,6,256]{2,1,0:T(8,128)(2,1)S(1)}, u32[]{:S(2)}, u32[]{:S(2)}) collective-permute-start(bf16[6,6,256]{2,1,0:T(8,128)(2,1)S(1)} %slice.48), channel_id=1, source_target_pairs={{0,15},{1,12},{2,13},{3,14},{4,3},{5,0},{6,1},{7,2},{8,7},{9,4},{1... | collective-permute-start | bytes 55304 | tf_op jit(solution)/shard_map/ppermute | solution.py:393
  10.6 34.8 %collective-permute-start.9 = (bf16[6,14,512]{2,1,0:T(8,128)(2,1)S(1)}, bf16[6,14,512]{2,1,0:T(8,128)(2,1)S(1)}, u32[]{:S(2)}, u32[]{:S(2)}) collective-permute-start(bf16[6,14,512]{2,1,0:T(8,128)(2,1)S(1)} %slice.52), channel_id=1, source_target_pairs={{0,12},{4,0},{8,4},{12,8},{1,13},{5,1},{9,5},{13,9},{2,14},{6,2},{... | collective-permute-start | bytes 258056 | tf_op jit(solution)/shard_map/ppermute | solution.py:385
  11.8 33.5 %collective-permute-start.10 = (bf16[7,6,512]{2,1,0:T(8,128)(2,1)S(1)}, bf16[7,6,512]{2,1,0:T(8,128)(2,1)S(1)}, u32[]{:S(2)}, u32[]{:S(2)}) collective-permute-start(bf16[7,6,512]{2,1,0:T(8,128)(2,1)S(1)} %slice.53), channel_id=1, source_target_pairs={{0,3},{1,0},{2,1},{3,2},{4,7},{5,4},{6,5},{7,6},{8,11},{9,8},{10,9... | collective-permute-start | bytes 129032 | tf_op jit(solution)/shard_map/ppermute | solution.py:385
  24.7 10.6 %collective-permute-start.3 = (bf16[192,256]{1,0:T(8,128)(2,1)}, bf16[192,256]{1,0:T(8,128)(2,1)S(1)}, u32[]{:S(2)}, u32[]{:S(2)}) collective-permute-start(bf16[192,256]{1,0:T(8,128)(2,1)} %get-tuple-element.40), channel_id=1, source_target_pairs={{0,4},{4,8},{8,12},{12,0},{1,5},{5,9},{9,13},{13,1},{2,6},{6,10},{... | collective-permute-start | bytes 294920 | tf_op jit(solution)/shard_map/ppermute | solution.py:385
  26.3 9.0 %collective-permute-start.4 = (bf16[224,256]{1,0:T(8,128)(2,1)}, bf16[224,256]{1,0:T(8,128)(2,1)S(1)}, u32[]{:S(2)}, u32[]{:S(2)}) collective-permute-start(bf16[224,256]{1,0:T(8,128)(2,1)} %get-tuple-element.41), channel_id=1, source_target_pairs={{0,1},{1,2},{2,3},{3,0},{4,5},{5,6},{6,7},{7,4},{8,9},{9,10},{10,1... | collective-permute-start | bytes 344072 | tf_op jit(solution)/shard_map/ppermute | solution.py:385
  26.5 6.4 %collective-permute-start.5 = (bf16[96,256]{1,0:T(8,128)(2,1)}, bf16[96,256]{1,0:T(8,128)(2,1)S(1)}, u32[]{:S(2)}, u32[]{:S(2)}) collective-permute-start(bf16[96,256]{1,0:T(8,128)(2,1)} %get-tuple-element.42), channel_id=1, source_target_pairs={{0,5},{1,6},{2,7},{3,4},{4,9},{5,10},{6,11},{7,8},{8,13},{9,14},{1... | collective-permute-start | bytes 147464 | tf_op jit(solution)/shard_map/ppermute | solution.py:393
  32.9 8.7 %collective-permute-start.11 = (bf16[6,6,512]{2,1,0:T(8,128)(2,1)S(1)}, bf16[6,6,512]{2,1,0:T(8,128)(2,1)S(1)}, u32[]{:S(2)}, u32[]{:S(2)}) collective-permute-start(bf16[6,6,512]{2,1,0:T(8,128)(2,1)S(1)} %slice.54), channel_id=1, source_target_pairs={{0,15},{1,12},{2,13},{3,14},{4,3},{5,0},{6,1},{7,2},{8,7},{9,4},{1... | collective-permute-start | bytes 110600 | tf_op jit(solution)/shard_map/ppermute | solution.py:393
  39.6 19.1 %copy-start.11 = (pred[112]{0:T(512)(128)(4,1)S(1)}, pred[112]{0:T(512)(128)(4,1)}, u32[]{:S(2)}) copy-start(pred[112]{0:T(512)(128)(4,1)} %constant.359.clone) | copy-start | bytes 340
  39.6 19.1 %copy-start.12 = (s32[112]{0:T(128)S(1)}, s32[112]{0:T(128)}, u32[]{:S(2)}) copy-start(s32[112]{0:T(128)} %constant.357.clone) | copy-start | bytes 1348
  39.6 19.1 %copy-start.13 = (s32[112]{0:T(128)S(1)}, s32[112]{0:T(128)}, u32[]{:S(2)}) copy-start(s32[112]{0:T(128)} %constant.358.clone) | copy-start | bytes 1348
  40.5 6.3 %collective-permute-start.7 = (bf16[112,512]{1,0:T(8,128)(2,1)}, bf16[112,512]{1,0:T(8,128)(2,1)S(1)}, u32[]{:S(2)}, u32[]{:S(2)}) collective-permute-start(bf16[112,512]{1,0:T(8,128)(2,1)} %get-tuple-element.44.tile), channel_id=1, source_target_pairs={{0,3},{1,0},{2,1},{3,2},{4,7},{5,4},{6,5},{7,6},{8,11},{9,8},{10,9... | collective-permute-start | bytes 344072 | tf_op jit(solution)/shard_map/ppermute | solution.py:385
  41.1 5.6 %collective-permute-start.6 = (bf16[96,512]{1,0:T(8,128)(2,1)S(1)}, bf16[96,512]{1,0:T(8,128)(2,1)S(1)}, u32[]{:S(2)}, u32[]{:S(2)}) collective-permute-start(bf16[96,512]{1,0:T(8,128)(2,1)S(1)} %slice.51), channel_id=1, source_target_pairs={{0,12},{4,0},{8,4},{12,8},{1,13},{5,1},{9,5},{13,9},{2,14},{6,2},{... | collective-permute-start | bytes 294920 | tf_op jit(solution)/shard_map/ppermute | solution.py:385
  41.6 5.2 %collective-permute-start.8 = (bf16[96,512]{1,0:T(8,128)(2,1)S(1)}, bf16[96,512]{1,0:T(8,128)(2,1)S(1)}, u32[]{:S(2)}, u32[]{:S(2)}) collective-permute-start(bf16[96,512]{1,0:T(8,128)(2,1)S(1)} %slice.51), channel_id=1, source_target_pairs={{0,15},{1,12},{2,13},{3,14},{4,3},{5,0},{6,1},{7,2},{8,7},{9,4},{1... | collective-permute-start | bytes 294920 | tf_op jit(solution)/shard_map/ppermute | solution.py:393
  56.6 13.9 %collective-permute-start.13 = (bf16[112,1024]{1,0:T(8,128)(2,1)}, bf16[112,1024]{1,0:T(8,128)(2,1)S(1)}, u32[]{:S(2)}, u32[]{:S(2)}) collective-permute-start(bf16[112,1024]{1,0:T(8,128)(2,1)} %get-tuple-element.47), channel_id=1, source_target_pairs={{0,1},{1,2},{2,3},{3,0},{4,5},{5,6},{6,7},{7,4},{8,9},{9,10},{10,1... | collective-permute-start | bytes 688136 | tf_op jit(solution)/shard_map/ppermute | solution.py:385
  57.8 9.8 %collective-permute-start.12 = (bf16[96,1024]{1,0:T(8,128)(2,1)}, bf16[96,1024]{1,0:T(8,128)(2,1)S(1)}, u32[]{:S(2)}, u32[]{:S(2)}) collective-permute-start(bf16[96,1024]{1,0:T(8,128)(2,1)} %get-tuple-element.46), channel_id=1, source_target_pairs={{0,4},{4,8},{8,12},{12,0},{1,5},{5,9},{9,13},{13,1},{2,6},{6,10},{... | collective-permute-start | bytes 589832 | tf_op jit(solution)/shard_map/ppermute | solution.py:385
  58.4 12.1 %collective-permute-start.14 = (bf16[96,1024]{1,0:T(8,128)(2,1)}, bf16[96,1024]{1,0:T(8,128)(2,1)S(1)}, u32[]{:S(2)}, u32[]{:S(2)}) collective-permute-start(bf16[96,1024]{1,0:T(8,128)(2,1)} %get-tuple-element.48), channel_id=1, source_target_pairs={{0,5},{1,6},{2,7},{3,4},{4,9},{5,10},{6,11},{7,8},{8,13},{9,14},{1... | collective-permute-start | bytes 589832 | tf_op jit(solution)/shard_map/ppermute | solution.py:393
  75.6 6.1 %collective-permute-start.16 = (bf16[224,256]{1,0:T(8,128)(2,1)}, bf16[224,256]{1,0:T(8,128)(2,1)S(1)}, u32[]{:S(2)}, u32[]{:S(2)}) collective-permute-start(bf16[224,256]{1,0:T(8,128)(2,1)} %get-tuple-element.54), channel_id=1, source_target_pairs={{0,3},{1,0},{2,1},{3,2},{4,7},{5,4},{6,5},{7,6},{8,11},{9,8},{10,9... | collective-permute-start | bytes 344072 | tf_op jit(solution)/shard_map/ppermute | solution.py:385
  76.5 5.2 %collective-permute-start.15 = (bf16[192,256]{1,0:T(8,128)(2,1)}, bf16[192,256]{1,0:T(8,128)(2,1)S(1)}, u32[]{:S(2)}, u32[]{:S(2)}) collective-permute-start(bf16[192,256]{1,0:T(8,128)(2,1)} %get-tuple-element.53), channel_id=1, source_target_pairs={{0,12},{4,0},{8,4},{12,8},{1,13},{5,1},{9,5},{13,9},{2,14},{6,2},{... | collective-permute-start | bytes 294920 | tf_op jit(solution)/shard_map/ppermute | solution.py:385
  77.0 4.1 %collective-permute-start.17 = (bf16[96,256]{1,0:T(8,128)(2,1)}, bf16[96,256]{1,0:T(8,128)(2,1)S(1)}, u32[]{:S(2)}, u32[]{:S(2)}) collective-permute-start(bf16[96,256]{1,0:T(8,128)(2,1)} %get-tuple-element.55), channel_id=1, source_target_pairs={{0,15},{1,12},{2,13},{3,14},{4,3},{5,0},{6,1},{7,2},{8,7},{9,4},{1... | collective-permute-start | bytes 147464 | tf_op jit(solution)/shard_map/ppermute | solution.py:393
  92.7 9.0 %collective-permute-start.18 = (bf16[192,256]{1,0:T(8,128)(2,1)}, bf16[192,256]{1,0:T(8,128)(2,1)S(1)}, u32[]{:S(2)}, u32[]{:S(2)}) collective-permute-start(bf16[192,256]{1,0:T(8,128)(2,1)} %get-tuple-element.60), channel_id=1, source_target_pairs={{0,4},{4,8},{8,12},{12,0},{1,5},{5,9},{9,13},{13,1},{2,6},{6,10},{... | collective-permute-start | bytes 294920 | tf_op jit(solution)/shard_map/ppermute | solution.py:385
  93.6 8.0 %collective-permute-start.19 = (bf16[224,256]{1,0:T(8,128)(2,1)}, bf16[224,256]{1,0:T(8,128)(2,1)S(1)}, u32[]{:S(2)}, u32[]{:S(2)}) collective-permute-start(bf16[224,256]{1,0:T(8,128)(2,1)} %get-tuple-element.61), channel_id=1, source_target_pairs={{0,1},{1,2},{2,3},{3,0},{4,5},{5,6},{6,7},{7,4},{8,9},{9,10},{10,1... | collective-permute-start | bytes 344072 | tf_op jit(solution)/shard_map/ppermute | solution.py:385
  93.6 8.0 %collective-permute-start.20 = (bf16[96,256]{1,0:T(8,128)(2,1)}, bf16[96,256]{1,0:T(8,128)(2,1)S(1)}, u32[]{:S(2)}, u32[]{:S(2)}) collective-permute-start(bf16[96,256]{1,0:T(8,128)(2,1)} %get-tuple-element.62), channel_id=1, source_target_pairs={{0,5},{1,6},{2,7},{3,4},{4,9},{5,10},{6,11},{7,8},{8,13},{9,14},{1... | collective-permute-start | bytes 147464 | tf_op jit(solution)/shard_map/ppermute | solution.py:393
  94.5 12.2 %copy-start.8 = (f32[1,512]{1,0:T(1,128)S(1)}, f32[1,512]{1,0:T(1,128)}, u32[]{:S(2)}) copy-start(f32[1,512]{1,0:T(1,128)} %get-tuple-element.66) | copy-start | bytes 6148
  94.5 14.1 %copy-start.1 = (bf16[1024,512]{1,0:T(8,128)(2,1)S(1)}, bf16[1024,512]{1,0:T(8,128)(2,1)}, u32[]{:S(2)}) copy-start(bf16[1024,512]{1,0:T(8,128)(2,1)} %get-tuple-element.68) | copy-start | bytes 3145732
  95.5 18.2 %collective-permute-start.26 = (bf16[4,2,16,1024]{3,2,1,0:T(8,128)(2,1)S(1)}, bf16[4,2,16,1024]{3,2,1,0:T(8,128)(2,1)}, u32[]{:S(2)}, u32[]{:S(2)}) collective-permute-start(bf16[4,2,16,1024]{3,2,1,0:T(8,128)(2,1)S(1)} %dynamic-slice_bitcast_fusion.4), channel_id=1, source_target_pairs={{0,1},{1,0},{2,3},{3,2},{4,5},{5,4},{6,7},{7,6},{8,9},{9,8},{10,11... | collective-permute-start | bytes 786440 | tf_op jit(solution)/shard_map/ppermute | solution.py:421
  103.0 12.5 %copy-start = (bf16[512,2048]{1,0:T(8,128)(2,1)S(1)}, bf16[512,2048]{1,0:T(8,128)(2,1)}, u32[]{:S(2)}) copy-start(bf16[512,2048]{1,0:T(8,128)(2,1)} %get-tuple-element.69) | copy-start | bytes 6291460
  106.7 1.2 collective-permute-start.21
  107.9 3.7 %collective-permute-start.22 = (f32[1,1792]{1,0:T(1,128)S(1)}, f32[1,1792]{1,0:T(1,128)S(1)}, u32[]{:S(2)}, u32[]{:S(2)}) collective-permute-start(f32[1,1792]{1,0:T(1,128)S(1)} %add.498), channel_id=1, source_target_pairs={{0,2},{1,3},{2,0},{3,1},{4,6},{5,7},{6,4},{7,5},{8,10},{9,11},{10,... | collective-permute-start | bytes 21512 | tf_op jit(solution)/shard_map/ppermute | solution.py:441
  108.6 16.3 %copy-start.2 = (bf16[1024,512]{1,0:T(8,128)(2,1)S(1)}, bf16[1024,512]{1,0:T(8,128)(2,1)}, u32[]{:S(2)}) copy-start(bf16[1024,512]{1,0:T(8,128)(2,1)} %get-tuple-element.68) | copy-start | bytes 3145732
  108.6 16.3 %collective-permute-start.31 = (bf16[4,2,64,512]{3,2,1,0:T(8,128)(2,1)S(1)}, bf16[4,2,64,512]{3,2,1,0:T(8,128)(2,1)S(1)}, u32[]{:S(2)}, u32[]{:S(2)}) collective-permute-start(bf16[4,2,64,512]{3,2,1,0:T(8,128)(2,1)S(1)} %dynamic-slice_bitcast_fusion.2), channel_id=1, source_target_pairs={{0,1},{1,0},{2,3},{3,2},{4,5},{5,4},{6,7},{7,6},{8,9},{9,8},{10,11... | collective-permute-start | bytes 1572872 | tf_op jit(solution)/shard_map/ppermute | solution.py:421
  111.6 4.9 %collective-permute-start.25 = (f32[1,1792]{1,0:T(1,128)S(1)}, f32[1,1792]{1,0:T(1,128)S(1)}, u32[]{:S(2)}, u32[]{:S(2)}) collective-permute-start(f32[1,1792]{1,0:T(1,128)S(1)} %add.499), channel_id=1, source_target_pairs={{0,12},{4,0},{8,4},{12,8},{1,13},{5,1},{9,5},{13,9},{2,14},{6,2},{... | collective-permute-start | bytes 21512 | tf_op jit(solution)/shard_map/ppermute | solution.py:385
  111.7 4.8 %collective-permute-start.24 = (f32[1,1792]{1,0:T(1,128)S(1)}, f32[1,1792]{1,0:T(1,128)S(1)}, u32[]{:S(2)}, u32[]{:S(2)}) collective-permute-start(f32[1,1792]{1,0:T(1,128)S(1)} %add.499), channel_id=1, source_target_pairs={{0,8},{4,12},{8,0},{12,4},{1,9},{5,13},{9,1},{13,5},{2,10},{6,14},... | collective-permute-start | bytes 21512 | tf_op jit(solution)/shard_map/ppermute | solution.py:385
  111.8 6.0 %collective-permute-start.23 = (f32[1,1792]{1,0:T(1,128)S(1)}, f32[1,1792]{1,0:T(1,128)S(1)}, u32[]{:S(2)}, u32[]{:S(2)}) collective-permute-start(f32[1,1792]{1,0:T(1,128)S(1)} %add.499), channel_id=1, source_target_pairs={{0,4},{4,8},{8,12},{12,0},{1,5},{5,9},{9,13},{13,1},{2,6},{6,10},{... | collective-permute-start | bytes 21512 | tf_op jit(solution)/shard_map/ppermute | solution.py:385
  114.8 5.0 %collective-permute-start.27 = (bf16[4,16,1024]{2,1,0:T(8,128)(2,1)S(1)}, bf16[4,16,1024]{2,1,0:T(8,128)(2,1)S(1)}, u32[]{:S(2)}, u32[]{:S(2)}) collective-permute-start(bf16[4,16,1024]{2,1,0:T(8,128)(2,1)S(1)} %dynamic-slice_bitcast_fusion.8), channel_id=1, source_target_pairs={{0,2},{1,3},{2,0},{3,1},{4,6},{5,7},{6,4},{7,5},{8,10},{9,11},{10,... | collective-permute-start | bytes 393224 | tf_op jit(solution)/shard_map/ppermute | solution.py:427
  116.5 12.9 %collective-permute-start.36 = (bf16[4,2,32,2048]{3,2,1,0:T(8,128)(2,1)}, bf16[4,2,32,2048]{3,2,1,0:T(8,128)(2,1)}, u32[]{:S(2)}, u32[]{:S(2)}) collective-permute-start(bf16[4,2,32,2048]{3,2,1,0:T(8,128)(2,1)} %dynamic-slice_bitcast_fusion), channel_id=1, source_target_pairs={{0,1},{1,0},{2,3},{3,2},{4,5},{5,4},{6,7},{7,6},{8,9},{9,8},{10,11... | collective-permute-start | bytes 3145736 | tf_op jit(solution)/shard_map/ppermute | solution.py:421
  119.9 5.8 %collective-permute-start.30 = (bf16[16,1024]{1,0:T(8,128)(2,1)S(1)}, bf16[16,1024]{1,0:T(8,128)(2,1)S(1)}, u32[]{:S(2)}, u32[]{:S(2)}) collective-permute-start(bf16[16,1024]{1,0:T(8,128)(2,1)S(1)} %get-tuple-element.77), channel_id=1, source_target_pairs={{0,12},{4,0},{8,4},{12,8},{1,13},{5,1},{9,5},{13,9},{2,14},{6,2},{... | collective-permute-start | bytes 98312 | tf_op jit(solution)/shard_map/ppermute | solution.py:385
  122.4 4.8 %collective-permute-start.29 = (bf16[16,1024]{1,0:T(8,128)(2,1)S(1)}, bf16[16,1024]{1,0:T(8,128)(2,1)S(1)}, u32[]{:S(2)}, u32[]{:S(2)}) collective-permute-start(bf16[16,1024]{1,0:T(8,128)(2,1)S(1)} %get-tuple-element.78), channel_id=1, source_target_pairs={{0,8},{4,12},{8,0},{12,4},{1,9},{5,13},{9,1},{13,5},{2,10},{6,14},... | collective-permute-start | bytes 98312 | tf_op jit(solution)/shard_map/ppermute | solution.py:385
  123.0 5.7 %collective-permute-start.28 = (bf16[16,1024]{1,0:T(8,128)(2,1)S(1)}, bf16[16,1024]{1,0:T(8,128)(2,1)S(1)}, u32[]{:S(2)}, u32[]{:S(2)}) collective-permute-start(bf16[16,1024]{1,0:T(8,128)(2,1)S(1)} %get-tuple-element.76), channel_id=1, source_target_pairs={{0,4},{4,8},{8,12},{12,0},{1,5},{5,9},{9,13},{13,1},{2,6},{6,10},{... | collective-permute-start | bytes 98312 | tf_op jit(solution)/shard_map/ppermute | solution.py:385
  125.1 7.9 %collective-permute-start.32 = (bf16[4,64,512]{2,1,0:T(8,128)(2,1)S(1)}, bf16[4,64,512]{2,1,0:T(8,128)(2,1)S(1)}, u32[]{:S(2)}, u32[]{:S(2)}) collective-permute-start(bf16[4,64,512]{2,1,0:T(8,128)(2,1)S(1)} %dynamic-slice_bitcast_fusion.3), channel_id=1, source_target_pairs={{0,2},{1,3},{2,0},{3,1},{4,6},{5,7},{6,4},{7,5},{8,10},{9,11},{10,... | collective-permute-start | bytes 786440 | tf_op jit(solution)/shard_map/ppermute | solution.py:427
  131.1 11.7 %collective-permute-start.37 = (bf16[4,32,2048]{2,1,0:T(8,128)(2,1)S(1)}, bf16[4,32,2048]{2,1,0:T(8,128)(2,1)S(1)}, u32[]{:S(2)}, u32[]{:S(2)}) collective-permute-start(bf16[4,32,2048]{2,1,0:T(8,128)(2,1)S(1)} %dynamic-slice_bitcast_fusion.1), channel_id=1, source_target_pairs={{0,2},{1,3},{2,0},{3,1},{4,6},{5,7},{6,4},{7,5},{8,10},{9,11},{10,... | collective-permute-start | bytes 1572872 | tf_op jit(solution)/shard_map/ppermute | solution.py:427
  133.1 12.3 %collective-permute-start.35 = (bf16[64,512]{1,0:T(8,128)(2,1)S(1)}, bf16[64,512]{1,0:T(8,128)(2,1)S(1)}, u32[]{:S(2)}, u32[]{:S(2)}) collective-permute-start(bf16[64,512]{1,0:T(8,128)(2,1)S(1)} %get-tuple-element.74), channel_id=1, source_target_pairs={{0,12},{4,0},{8,4},{12,8},{1,13},{5,1},{9,5},{13,9},{2,14},{6,2},{... | collective-permute-start | bytes 196616 | tf_op jit(solution)/shard_map/ppermute | solution.py:385
  136.1 9.4 %collective-permute-start.34 = (bf16[64,512]{1,0:T(8,128)(2,1)S(1)}, bf16[64,512]{1,0:T(8,128)(2,1)S(1)}, u32[]{:S(2)}, u32[]{:S(2)}) collective-permute-start(bf16[64,512]{1,0:T(8,128)(2,1)S(1)} %get-tuple-element.75), channel_id=1, source_target_pairs={{0,8},{4,12},{8,0},{12,4},{1,9},{5,13},{9,1},{13,5},{2,10},{6,14},... | collective-permute-start | bytes 196616 | tf_op jit(solution)/shard_map/ppermute | solution.py:385
  136.3 9.3 %collective-permute-start.33 = (bf16[64,512]{1,0:T(8,128)(2,1)S(1)}, bf16[64,512]{1,0:T(8,128)(2,1)S(1)}, u32[]{:S(2)}, u32[]{:S(2)}) collective-permute-start(bf16[64,512]{1,0:T(8,128)(2,1)S(1)} %get-tuple-element.73), channel_id=1, source_target_pairs={{0,4},{4,8},{8,12},{12,0},{1,5},{5,9},{9,13},{13,1},{2,6},{6,10},{... | collective-permute-start | bytes 196616 | tf_op jit(solution)/shard_map/ppermute | solution.py:385
  143.0 7.3 %collective-permute-start.40 = (bf16[32,2048]{1,0:T(8,128)(2,1)S(1)}, bf16[32,2048]{1,0:T(8,128)(2,1)S(1)}, u32[]{:S(2)}, u32[]{:S(2)}) collective-permute-start(bf16[32,2048]{1,0:T(8,128)(2,1)S(1)} %get-tuple-element.71), channel_id=1, source_target_pairs={{0,12},{4,0},{8,4},{12,8},{1,13},{5,1},{9,5},{13,9},{2,14},{6,2},{... | collective-permute-start | bytes 393224 | tf_op jit(solution)/shard_map/ppermute | solution.py:385
  144.9 10.0 %collective-permute-start.39 = (bf16[32,2048]{1,0:T(8,128)(2,1)S(1)}, bf16[32,2048]{1,0:T(8,128)(2,1)S(1)}, u32[]{:S(2)}, u32[]{:S(2)}) collective-permute-start(bf16[32,2048]{1,0:T(8,128)(2,1)S(1)} %get-tuple-element.72), channel_id=1, source_target_pairs={{0,8},{4,12},{8,0},{12,4},{1,9},{5,13},{9,1},{13,5},{2,10},{6,14},... | collective-permute-start | bytes 393224 | tf_op jit(solution)/shard_map/ppermute | solution.py:385
  145.4 9.5 %collective-permute-start.38 = (bf16[32,2048]{1,0:T(8,128)(2,1)S(1)}, bf16[32,2048]{1,0:T(8,128)(2,1)S(1)}, u32[]{:S(2)}, u32[]{:S(2)}) collective-permute-start(bf16[32,2048]{1,0:T(8,128)(2,1)S(1)} %get-tuple-element.70), channel_id=1, source_target_pairs={{0,4},{4,8},{8,12},{12,0},{1,5},{5,9},{9,13},{13,1},{2,6},{6,10},{... | collective-permute-start | bytes 393224 | tf_op jit(solution)/shard_map/ppermute | solution.py:385
  (31 other events, 142.1 us)

commit v2 on v1

v2 whole, which is shorter than its diff:
```python
import functools

import jax
import jax.numpy as jnp
import numpy as np
from jax import lax
from jax.experimental import pallas as pl
from jax.experimental.pallas import tpu as pltpu
from jax.sharding import PartitionSpec as P

HEAD = 32
WIN = 7
MARGIN = WIN - 1
SLOT = 64
PM = 16
LANES = 128
EPSILON = 1e-05
MASKED = -100.0
F32 = jnp.float32
BF16 = jnp.bfloat16


def pitch_of(count):
    return -(-count // 16) * 16


def window_tokens(rows, cols):
    h, w, ok = [], [], []
    for wr in range(rows // WIN):
        for wc in range(cols // WIN):
            for t in range(SLOT):
                good = t < WIN * WIN
                h.append(wr * WIN + t // WIN if good else 0)
                w.append(wc * WIN + t % WIN if good else 0)
                ok.append(good)
    return np.array(h, np.int32), np.array(w, np.int32), np.array(ok)


def grid_tokens(rows, cols, pitch):
    h = np.repeat(np.arange(rows, dtype=np.int32), pitch)
    w = np.tile(np.arange(pitch, dtype=np.int32), rows)
    ok = w < cols
    return h, np.where(ok, w, 0).astype(np.int32), ok


def quad_tokens(rows, cols):
    a, b, ok = grid_tokens(rows // 2, cols // 2, pitch_of(cols // 2))
    h = np.concatenate([2 * a + (k & 1) for k in range(4)])
    w = np.concatenate([2 * b + (k >> 1) for k in range(4)])
    return h, w, np.tile(ok, 4)


def win_index(h, w, cols):
    return ((h // WIN) * (cols // WIN) + w // WIN) * SLOT + (h % WIN) * WIN + w % WIN


def quad_index(h, w, rows, cols):
    pitch = pitch_of(cols // 2)
    return ((h % 2) + 2 * (w % 2)) * ((rows // 2) * pitch) + (h // 2) * pitch + w // 2


def ahead_index(h, w, ok, shift_rows, shift_cols, rows, cols, inner, base):
    pitch = pitch_of(cols)
    h2, w2 = h + shift_rows, w + shift_cols
    local = inner(jnp.minimum(h2, rows - 1), jnp.minimum(w2, cols - 1))
    below = base + (h2 - rows) * pitch + w2
    side = base + MARGIN * pitch + h2 * PM + (w2 - cols)
    idx = jnp.where(w2 >= cols, side, jnp.where(h2 >= rows, below, local))
    return jnp.where(ok, idx, -1).astype(jnp.int32).reshape(-1, 1)


def behind_index(h, w, ok, shift_rows, shift_cols, rows, cols, base):
    pitch = pitch_of(cols)
    h2, w2 = h - shift_rows, w - shift_cols
    local = win_index(jnp.maximum(h2, 0), jnp.maximum(w2, 0), cols)
    above = base + (h2 + MARGIN) * pitch + w2
    row = jnp.where(h2 >= 0, h2, rows + h2 + MARGIN)
    side = base + MARGIN * pitch + row * PM + (w2 + MARGIN)
    idx = jnp.where(w2 < 0, side, jnp.where(h2 < 0, above, local))
    return jnp.where(ok, idx, -1).astype(jnp.int32).reshape(-1, 1)


def piece_index(rows, cols, inner, first):
    top = 0 if first else rows - MARGIN
    left = 0 if first else cols - MARGIN
    parts = []
    for count, wide, pitch, h0, w0 in (
        (MARGIN, cols, pitch_of(cols), top, 0),
        (rows, MARGIN, PM, 0, left),
    ):
        h, w, ok = grid_tokens(count, wide, pitch)
        parts.append(np.where(ok, inner(h + h0, w + w0), -1))
    return np.concatenate(parts).astype(np.int32).reshape(-1, 1)


def window_labels(rows, cols, axis_row, axis_col, shift_rows, shift_cols):
    h, w, ok = window_tokens(rows, cols)
    height = rows * lax.axis_size("rows")
    breadth = cols * lax.axis_size("cols")
    gh = axis_row * rows + h
    gw = axis_col * cols + w
    lh = jnp.where(gh < height - WIN, 0, jnp.where(gh < height - shift_rows, 1, 2))
    lw = jnp.where(gw < breadth - WIN, 0, jnp.where(gw < breadth - shift_cols, 1, 2))
    flat = jnp.where(ok, lh * 3 + lw, -1).astype(jnp.int32)
    return flat.reshape(-1, 1), flat.reshape(-1, SLOT)


def dot(a, b):
    return jnp.dot(a, b, preferred_element_type=F32)


def dot_nt(a, b):
    return lax.dot_general(a, b, (((1,), (1,)), ((), ())), preferred_element_type=F32)


def dot_tn(a, b):
    return lax.dot_general(a, b, (((0,), (0,)), ((), ())), preferred_element_type=F32)


def select(idx, source):
    count = source.shape[0]
    lane = lax.broadcasted_iota(jnp.int32, (idx.shape[0], count), 1)
    hot = jnp.where(idx == lane, 1.0, 0.0).astype(BF16)
    return dot(hot, source).astype(BF16)


def norm_parts(x):
    centred = x - jnp.mean(x, axis=-1, keepdims=True)
    inverse = lax.rsqrt(jnp.mean(centred * centred, axis=-1, keepdims=True) + EPSILON)
    return centred * inverse, inverse


def norm_back(hat, inverse, gain, dy):
    grad_gain = jnp.sum(dy * hat, axis=0, keepdims=True)
    t = dy * gain
    dx = inverse * (
        t
        - jnp.mean(t, axis=-1, keepdims=True)
        - hat * jnp.mean(t * hat, axis=-1, keepdims=True)
    )
    return dx.astype(BF16), grad_gain


PACK = LANES // HEAD


def head_masks():
    lane = lax.broadcasted_iota(jnp.int32, (1, LANES), 1) // HEAD
    return [jnp.where(lane == h, 1.0, 0.0).astype(BF16) for h in range(PACK)]


def stack_heads(x, masks):
    return jnp.concatenate([x * m for m in masks], axis=0)


def pick_heads(o):
    lane = lax.broadcasted_iota(jnp.int32, (SLOT, LANES), 1) // HEAD
    out = o[:SLOT]
    for h in range(1, PACK):
        out = jnp.where(lane == h, o[h * SLOT : (h + 1) * SLOT], out)
    return out


def window_bias(lc_ref, lr_ref, w):
    lc = lc_ref[w * SLOT : (w + 1) * SLOT, :]
    lr = lr_ref[w : w + 1, :]
    bias = jnp.where((lc == lr) | (lc < 0), 0.0, MASKED)
    bias = jnp.where(lr < 0, -1e30, bias)
    return jnp.concatenate([bias] * PACK, axis=0)


def soft(qs, k, bias):
    raised = jnp.exp(dot_nt(qs, k) * HEAD ** (-0.5) + bias)
    return raised * (1.0 / jnp.sum(raised, axis=-1, keepdims=True))


def unit_back(qs, k, v, weights, wb, dm, masks):
    dms = stack_heads(dm, masks)
    dw = dot_nt(dms, v).astype(BF16).astype(F32)
    ds = weights * (dw - jnp.sum(dw * weights, axis=-1, keepdims=True))
    ds = (ds * HEAD ** (-0.5)).astype(BF16)
    dq = pick_heads(dot(ds, k))
    dk = dot_tn(ds, qs)
    dv = dot_tn(wb, dms)
    return dq.astype(BF16), dk.astype(BF16), dv.astype(BF16)


def fill_tile(scratch, tile, pitch):
    count, wide, _ = tile.shape
    for r in range(count):
        scratch[r * pitch : r * pitch + wide, :] = tile[r]


class Bag:
    pass


MESH = pl.DeviceIdType.MESH


class Links:
    def __init__(self, send, recv):
        self.send, self.recv, self.used = send, recv, 0
        self.group = lax.axis_index("groups")
        self.row, self.col = lax.axis_index("rows"), lax.axis_index("cols")
        self.nr, self.nc = lax.axis_size("rows"), lax.axis_size("cols")
        self.core, self.chip = lax.rem(self.col, 2), self.col // 2
        self.chips = self.nc // 2

    def device(self, dr, dc):
        row = lax.rem(self.row + dr + self.nr, self.nr)
        col = lax.rem(self.col + dc + self.nc, self.nc)
        return (self.group, row, col)

    def partner(self):
        return (self.group, self.row, self.chip * 2 + 1 - self.core)

    def barrier(self):
        offsets = {(d, 0) for d in range(1, self.nr)} | {(0, d) for d in range(1, self.nc)}
        offsets |= {(1, 1), (self.nr - 1, self.nc - 1)}
        sem = pltpu.get_barrier_semaphore()
        for dr, dc in sorted(offsets):
            pl.semaphore_signal(sem, inc=1, device_id=self.device(dr, dc), device_id_type=MESH)
        pl.semaphore_wait(sem, len(offsets))

    def start(self, source, target, device):
        copy = pltpu.make_async_remote_copy(
            src_ref=source,
            dst_ref=target,
            send_sem=self.send.at[self.used],
            recv_sem=self.recv.at[self.used],
            device_id=device,
            device_id_type=MESH,
        )
        self.used += 1
        copy.start()
        return copy

    def exchange(self, row, col, corner, halo, by):
        return [
            self.start(row, halo[0], self.device(by, 0)),
            self.start(col, halo[1], self.device(0, by)),
            self.start(corner, halo[2], self.device(by, by)),
        ]


def wait_all(copies):
    for copy in copies:
        copy.wait()


class Reduction:
    def __init__(self, links, kind, parts, bufs):
        self.links, self.kind, self.parts = links, kind, parts
        self.got1, self.half, self.got2, self.part, self.got3 = bufs

    def first(self):
        k = self.links
        self.copies = [k.start(self.parts.at[1 - k.core], self.got1, k.partner())]

    def second(self):
        k = self.links
        wait_all(self.copies)
        for x in range(k.chips):
            for r in range(k.nr):
                total = self.parts[k.core, x, r].astype(F32) + self.got1[x, r].astype(F32)
                self.half[x, r] = total.astype(self.kind)
        self.copies = [
            k.start(self.half.at[lax.rem(k.chip + d, k.chips)], self.got2.at[d - 1], k.device(0, 2 * d))
            for d in range(1, k.chips)
        ]

    def third(self):
        k = self.links
        wait_all(self.copies)
        for r in range(k.nr):
            total = self.half[k.chip, r].astype(F32)
            for d in range(1, k.chips):
                total = total + self.got2[d - 1, r].astype(F32)
            self.part[r] = total.astype(self.kind)
        self.copies = [
            k.start(self.part.at[lax.rem(k.row + d, k.nr)], self.got3.at[d - 1], k.device(d, 0))
            for d in range(1, k.nr)
        ]

    def finish(self):
        k = self.links
        wait_all(self.copies)
        total = self.part[k.row].astype(F32)
        for d in range(1, k.nr):
            total = total + self.got3[d - 1].astype(F32)
        return total


class GainSum:
    def __init__(self, links, bufs):
        self.links = links
        self.own, self.got1, self.half, self.got2, self.part, self.got3 = bufs

    def first(self):
        self.copies = [self.links.start(self.own, self.got1, self.links.partner())]

    def second(self):
        k = self.links
        wait_all(self.copies)
        self.half[...] = self.own[...] + self.got1[...]
        self.copies = [
            k.start(self.half, self.got2.at[d - 1], k.device(0, 2 * d)) for d in range(1, k.chips)
        ]

    def third(self):
        k = self.links
        wait_all(self.copies)
        total = self.half[...]
        for d in range(1, k.chips):
            total = total + self.got2[d - 1]
        self.part[...] = total
        self.copies = [k.start(self.part, self.got3.at[d - 1], k.device(d, 0)) for d in range(1, k.nr)]

    def finish(self):
        wait_all(self.copies)
        total = self.part[...]
        for d in range(1, self.links.nr):
            total = total + self.got3[d - 1]
        return total


def store_parts(parts, value, offset):
    _, chips, nr, depth, _ = parts.shape
    width = value.shape[1]
    for r in range(nr):
        for x in range(chips):
            for core in range(2):
                i = (r * chips + x) * 2 + core
                piece = value[i * depth : (i + 1) * depth]
                parts[core, x, r, :, offset : offset + width] = piece.astype(BF16)


def fill_side(scratch, tile):
    scratch[...] = jnp.zeros_like(scratch)
    for r in range(tile.shape[0]):
        scratch[r * PM : r * PM + MARGIN, :] = tile[r, :MARGIN, :]


def put_pieces(idx, source, row_ref, col_ref):
    got = select(idx[...], source)
    row_ref[...] = got[: row_ref.shape[0]]
    col_ref[...] = got[row_ref.shape[0] :]


def lanes_of(width, g):
    return [slice(t * width + g * LANES, t * width + (g + 1) * LANES) for t in range(3)]


def joined_ext(first, halo):
    return jnp.concatenate([first] + [h[...] for h in halo], axis=0)


def whole_kernel(in_names, out_names, scratch_names, *refs):
    b = Bag()
    for name, ref in zip(in_names + out_names + scratch_names, refs, strict=True):
        setattr(b, name, ref)
    links = Links(b.send, b.recv)
    rows, cols, narrow = b.tok.shape
    rows3, cols3, wide = b.cot.shape
    pitch, pitch3 = pitch_of(cols), pitch_of(cols3)
    red3 = Reduction(links, BF16, b.g3, [getattr(b, f"g3_{i}") for i in range(5)])
    redm = Reduction(links, BF16, b.gm, [getattr(b, f"gm_{i}") for i in range(5)])
    red2 = Reduction(links, BF16, b.g2, [getattr(b, f"g2_{i}") for i in range(5)])
    redg = GainSum(links, [getattr(b, f"gg_{i}") for i in range(6)])
    halos = [[getattr(b, f"h{n}_{i}") for i in range(3)] for n in range(7)]
    margin2 = slice(0, MARGIN * PM)
    masks = head_masks()

    b.toks[...] = jnp.zeros_like(b.toks)
    fill_tile(b.toks, b.tok, pitch)
    fill_side(b.tside, b.tok)
    b.cots[...] = jnp.zeros_like(b.cots)
    fill_tile(b.cots, b.cot, pitch3)
    fill_side(b.cside, b.cot)
    links.barrier()
    flying = links.exchange(
        b.toks.at[0 : MARGIN * pitch], b.tside, b.tside.at[margin2], halos[0], -1
    )
    flying_c = links.exchange(
        b.cots.at[0 : MARGIN * pitch3], b.cside, b.cside.at[margin2], halos[1], -1
    )

    quad = select(b.idx_q[...], b.toks[...])
    wait_all(flying)
    hat, _ = norm_parts(select(b.idx_a[...], joined_ext(b.toks[...], halos[0])).astype(F32))
    b.rolled[...] = (hat * b.gain2[...]).astype(BF16)
    b.packed[...] = dot(b.rolled[...], b.qkv2[...]).astype(BF16)
    for w in range(b.lr2.shape[0]):
        bias = window_bias(b.lc2, b.lr2, w)
        at = slice(w * SLOT, (w + 1) * SLOT)
        for g in range(narrow // LANES):
            lanes = lanes_of(narrow, g)
            qs = stack_heads(b.packed[at, lanes[0]], masks)
            wb = soft(qs, b.packed[at, lanes[1]], bias).astype(BF16)
            b.mixed[at, lanes[0]] = pick_heads(dot(wb, b.packed[at, lanes[2]])).astype(BF16)
    win = dot(b.mixed[...], b.proj2[...]).astype(BF16)
    put_pieces(b.idx_b, win, b.row1, b.col1)
    last2 = slice((rows - MARGIN) * PM, rows * PM)
    flying = links.exchange(b.row1, b.col1, b.col1.at[last2], halos[2], 1)

    wait_all(flying)
    restored = select(b.idx_c[...], joined_ext(win, halos[2]))
    section = (quad.astype(F32) + restored.astype(F32)).astype(BF16)
    t3 = rows3 * pitch3
    joined = jnp.concatenate([section[k * t3 : (k + 1) * t3] for k in range(4)], axis=1)
    b.joined[...] = joined
    hat, _ = norm_parts(joined.astype(F32))
    b.mnorm[...] = (hat * b.gainm[...]).astype(BF16)
    b.merged[...] = dot(b.mnorm[...], b.weight[...]).astype(BF16)
    hat, _ = norm_parts(b.merged[...].astype(F32))
    normed3 = (hat * b.gain3[...]).astype(BF16)
    b.normed3[...] = normed3
    for r in range(rows3):
        b.nside[r * PM : (r + 1) * PM, :] = normed3[r * pitch3 : r * pitch3 + PM]
    flying = links.exchange(
        b.normed3.at[0 : MARGIN * pitch3], b.nside, b.nside.at[margin2], halos[3], -1
    )

    wait_all(flying_c)
    dproj = select(b.idx_d[...], joined_ext(b.cots[...], halos[1]))
    dmixed = dot_nt(dproj, b.proj3[...]).astype(BF16)
    wait_all(flying)
    rolled3 = select(b.idx_d[...], joined_ext(b.normed3[...], halos[3]))
    b.packed3[...] = dot(rolled3, b.qkv3[...]).astype(BF16)
    for w in range(b.lr3.shape[0]):
        bias = window_bias(b.lc3, b.lr3, w)
        at = slice(w * SLOT, (w + 1) * SLOT)
        for g in range(wide // LANES):
            lanes = lanes_of(wide, g)
            qs = stack_heads(b.packed3[at, lanes[0]], masks)
            k, v = b.packed3[at, lanes[1]], b.packed3[at, lanes[2]]
            weights = soft(qs, k, bias)
            wb = weights.astype(BF16)
            b.mixed3[at, lanes[0]] = pick_heads(dot(wb, v)).astype(BF16)
            back = unit_back(qs, k, v, weights, wb, dmixed[at, lanes[0]], masks)
            for t in range(3):
                b.dpacked3[at, lanes[t]] = back[t]
    b.both[:, :wide] = dot(b.mixed3[...], b.proj3[...]).astype(BF16)
    b.both[:, wide:] = dot_nt(b.dpacked3[...], b.qkv3[...]).astype(BF16)
    put_pieces(b.idx_e, b.both[...], b.row2, b.col2)
    last3 = slice((rows3 - MARGIN) * PM, rows3 * PM)
    flying = links.exchange(b.row2, b.col2, b.col2.at[last3], halos[4], 1)
    store_parts(b.g3, dot_tn(rolled3, b.dpacked3[...]), 0)
    store_parts(b.g3, dot_tn(b.mixed3[...], dproj), 3 * wide)
    red3.first()

    wait_all(flying)
    back = select(b.idx_f[...], joined_ext(b.both[...], halos[4]))
    mine = b.merged[...].astype(F32)
    total = (mine + back[:, :wide].astype(F32)).astype(BF16)
    for r in range(rows3):
        b.out[r] = total[r * pitch3 : r * pitch3 + cols3]
    hat, inv = norm_parts(mine)
    dmerged, grad3 = norm_back(hat, inv, b.gain3[...], back[:, wide:].astype(F32))
    dmerged = b.cots[...] + dmerged
    hat, inv = norm_parts(b.joined[...].astype(F32))
    djn = dot_nt(dmerged, b.weight[...]).astype(BF16).astype(F32)
    djoined, gradm = norm_back(hat, inv, b.gainm[...], djn)
    b.gg_0[:, narrow : 5 * narrow] = gradm
    b.gg_0[:, 5 * narrow :] = grad3
    b.dsec[...] = jnp.concatenate(
        [djoined[:, k * narrow : (k + 1) * narrow] for k in range(4)], axis=0
    )
    put_pieces(b.idx_g, b.dsec[...], b.row3, b.col3)
    flying = links.exchange(b.row3, b.col3, b.col3.at[margin2], halos[5], -1)
    store_parts(b.gm, dot_tn(b.mnorm[...], dmerged), 0)
    redm.first()

    wait_all(flying)
    red3.second()
    dproj = select(b.idx_h[...], joined_ext(b.dsec[...], halos[5]))
    dmixed = dot_nt(dproj, b.proj2[...]).astype(BF16)
    for w in range(b.lr2.shape[0]):
        bias = window_bias(b.lc2, b.lr2, w)
        at = slice(w * SLOT, (w + 1) * SLOT)
        for g in range(narrow // LANES):
            lanes = lanes_of(narrow, g)
            qs = stack_heads(b.packed[at, lanes[0]], masks)
            k, v = b.packed[at, lanes[1]], b.packed[at, lanes[2]]
            weights = soft(qs, k, bias)
            back = unit_back(
                qs, k, v, weights, weights.astype(BF16), dmixed[at, lanes[0]], masks
            )
            for t in range(3):
                b.dpacked[at, lanes[t]] = back[t]
    drolled = dot_nt(b.dpacked[...], b.qkv2[...]).astype(BF16)
    put_pieces(b.idx_b, drolled, b.row4, b.col4)
    flying = links.exchange(b.row4, b.col4, b.col4.at[last2], halos[6], 1)
    store_parts(b.g2, dot_tn(b.rolled[...], b.dpacked[...]), 0)
    store_parts(b.g2, dot_tn(b.mixed[...], dproj), 3 * narrow)
    red2.first()
    red3.third()
    redm.second()

    wait_all(flying)
    dnormed = select(b.idx_i[...], joined_ext(drolled, halos[6])).astype(F32)
    hat, inv = norm_parts(b.toks[...].astype(F32))
    dtok, grad2 = norm_back(hat, inv, b.gain2[...], dnormed)
    b.gg_0[:, :narrow] = grad2
    redg.first()
    red2.second()
    total = select(b.idx_n[...], b.dsec[...]) + dtok
    for r in range(rows):
        b.dtok[r] = total[r * pitch : r * pitch + cols]
    redg.second()
    redm.third()
    red2.third()
    redg.third()
    b.sum3[...] = red3.finish().astype(BF16)
    b.summ[...] = redm.finish().astype(BF16)
    b.sum2[...] = red2.finish().astype(BF16)
    b.gains[...] = redg.finish()


def on_device(
    tokens, cotangent, shifts, norm2_gain, qkv2, proj2, merge_gain, merge_weight, norm3_gain,
    qkv3, proj3,
):
    rows, cols, narrow = tokens.shape
    wide = qkv3.shape[0]
    rows3, cols3 = rows // 2, cols // 2
    pitch, pitch3 = pitch_of(cols), pitch_of(cols3)
    base, base3 = rows * pitch, rows3 * pitch3
    r, c = lax.axis_index("rows"), lax.axis_index("cols")
    s0, s1, s2, s3 = shifts[0], shifts[1], shifts[2], shifts[3]

    win2, win3 = window_tokens(rows, cols), window_tokens(rows3, cols3)
    n2, n3 = len(win2[0]), len(win3[0])
    quad = quad_tokens(rows, cols)
    nat = grid_tokens(rows, cols, pitch)
    grid3 = grid_tokens(rows3, cols3, pitch3)
    as_grid = lambda h, w: h * pitch + w
    as_grid3 = lambda h, w: h * pitch3 + w
    as_quad = lambda h, w: quad_index(h, w, rows, cols)
    as_win = lambda h, w: win_index(h, w, cols)
    as_win3 = lambda h, w: win_index(h, w, cols3)
    fixed = lambda t, inner: np.where(t[2], inner(t[0], t[1]), -1).astype(np.int32).reshape(-1, 1)

    idx_a = ahead_index(*win2, s0, s1, rows, cols, as_grid, base)
    idx_h = ahead_index(*win2, s0, s1, rows, cols, as_quad, len(quad[0]))
    idx_d = ahead_index(*win3, s2, s3, rows3, cols3, as_grid3, base3)
    idx_c = behind_index(*quad, s0, s1, rows, cols, n2)
    idx_i = behind_index(*nat, s0, s1, rows, cols, n2)
    idx_f = behind_index(*grid3, s2, s3, rows3, cols3, n3)
    idx_q = fixed(quad, as_grid)
    idx_n = fixed(nat, as_quad)
    idx_b = piece_index(rows, cols, as_win, False)
    idx_e = piece_index(rows3, cols3, as_win3, False)
    idx_g = piece_index(rows, cols, as_quad, True)
    lc2, lr2 = window_labels(rows, cols, r, c, s0, s1)
    lc3, lr3 = window_labels(rows3, cols3, r, c, s2, s3)
    gain2, gainm, gain3 = (g.reshape(1, -1) for g in (norm2_gain, merge_gain, norm3_gain))
    nr, nc = lax.axis_size("rows"), lax.axis_size("cols")
    chips = nc // 2
    quads, gains = len(quad[0]), 5 * narrow + wide
    inputs = dict(
        tok=tokens, cot=cotangent, idx_a=idx_a, idx_b=idx_b, idx_c=idx_c, idx_d=idx_d, idx_e=idx_e,
        idx_f=idx_f, idx_g=idx_g, idx_h=idx_h, idx_i=idx_i, idx_n=idx_n, idx_q=idx_q, lc2=lc2,
        lr2=lr2, lc3=lc3, lr3=lr3, gain2=gain2, gainm=gainm, gain3=gain3, qkv2=qkv2, proj2=proj2,
        weight=merge_weight, qkv3=qkv3, proj3=proj3,
    )
    m3, mm, m2 = wide // (nr * nc), 4 * narrow // (nr * nc), narrow // (nr * nc)
    outs = dict(
        out=(cotangent.shape, BF16),
        dtok=(tokens.shape, BF16),
        gains=((1, gains), F32),
        sum3=((m3, 4 * wide), BF16),
        summ=((mm, wide), BF16),
        sum2=((m2, 4 * narrow), BF16),
    )
    row2, col2, cor = MARGIN * pitch, rows * PM, MARGIN * PM
    row3, col3 = MARGIN * pitch3, rows3 * PM
    scratch = dict(
        toks=((base, narrow), BF16), tside=((col2, narrow), BF16),
        cots=((base3, wide), BF16), cside=((col3, wide), BF16),
        rolled=((n2, narrow), BF16), packed=((n2, 3 * narrow), BF16), mixed=((n2, narrow), BF16),
        joined=((base3, 4 * narrow), BF16), mnorm=((base3, 4 * narrow), BF16),
        merged=((base3, wide), BF16), normed3=((base3, wide), BF16), nside=((col3, wide), BF16),
        packed3=((n3, 3 * wide), BF16), mixed3=((n3, wide), BF16),
        dpacked3=((n3, 3 * wide), BF16), both=((n3, 2 * wide), BF16),
        dsec=((quads, narrow), BF16), dpacked=((n2, 3 * narrow), BF16),
        row1=((row2, narrow), BF16), col1=((col2, narrow), BF16),
        row2=((row3, 2 * wide), BF16), col2=((col3, 2 * wide), BF16),
        row3=((row2, narrow), BF16), col3=((col2, narrow), BF16),
        row4=((row2, narrow), BF16), col4=((col2, narrow), BF16),
    )
    copies = 7 * 3
    for n, (big, width) in enumerate(
        ((1, narrow), (0, wide), (1, narrow), (0, wide), (0, 2 * wide), (1, narrow), (1, narrow))
    ):
        for i, size in enumerate((row2, col2, cor) if big else (row3, col3, cor)):
            scratch[f"h{n}_{i}"] = ((size, width), BF16)
    for name, shape in (("g3", (m3, 4 * wide)), ("gm", (mm, wide)), ("g2", (m2, 4 * narrow))):
        scratch[name] = ((2, chips, nr) + shape, BF16)
        for i, lead in enumerate(
            ((chips, nr), (chips, nr), (max(chips - 1, 1), nr), (nr,), (max(nr - 1, 1),))
        ):
            scratch[f"{name}_{i}"] = (lead + shape, BF16)
        copies += chips + nr - 1
    for i, lead in enumerate(((), (), (), (max(chips - 1, 1),), (), (max(nr - 1, 1),))):
        scratch[f"gg_{i}"] = (lead + (1, gains), F32)
    copies += chips + nr - 1
    spaces = [pltpu.VMEM(s, d) for s, d in scratch.values()]
    spaces += [pltpu.SemaphoreType.DMA((copies,)), pltpu.SemaphoreType.DMA((copies,))]
    out, tokens_grad, total, sum3, sum_m, sum2 = pl.pallas_call(
        functools.partial(
            whole_kernel, list(inputs), list(outs), list(scratch) + ["send", "recv"]
        ),
        out_shape=[jax.ShapeDtypeStruct(s, d) for s, d in outs.values()],
        in_specs=[pl.BlockSpec(memory_space=pltpu.VMEM)] * len(inputs),
        out_specs=[pl.BlockSpec(memory_space=pltpu.VMEM)] * len(outs),
        scratch_shapes=spaces,
        compiler_params=pltpu.CompilerParams(
            collective_id=0, has_side_effects=True, vmem_limit_bytes=60 * 2**20
        ),
        name="block",
    )(*inputs.values())
    return (
        out,
        tokens_grad,
        total.reshape(-1),
        sum2[:, : 3 * narrow].reshape(-1),
        sum2[:, 3 * narrow :].reshape(-1),
        sum_m.reshape(-1),
        sum3[:, : 3 * wide].reshape(-1),
        sum3[:, 3 * wide :].reshape(-1),
    )


def solution(mesh):
    tile = P(("groups", "rows"), "cols", None)
    spread = P(("groups", "rows", "cols"))
    return jax.shard_map(
        on_device,
        mesh=mesh,
        in_specs=(tile, tile) + (P(),) * 9,
        out_specs=(tile, tile, P("groups")) + (spread,) * 5,
        check_vma=False,
    )
```

time: 157 us -> 122 us (0.78)
  Pallas kernels: 34.8 us -> 89 us
  waiting for transfers between devices: 44.4 us -> 0 us
  starting transfers between devices: 37.1 us -> 0 us
  local copies, waits for them, and re-layouts: 26.8 us -> 19.6 us
    pallas_call x6 -> x1, Pallas kernels: 34.8 us -> 89 us  [on_device(): pl.pallas_call(functools.partial(whole_kernel, list(inputs), list(outs),...]
    ppermute x41 -> x0, waiting for transfers between devices: 44.4 us -> none  [the longest x26 21.9 us: passed_along(): lax.ppermute(value, axis, [(i, (i + by) % count) for i in range(count)])]
    ppermute x41 -> x0, starting transfers between devices: 37.1 us -> none  [the longest x26 26.5 us: passed_along(): lax.ppermute(value, axis, [(i, (i + by) % count) for i in range(count)])]
    slice x7 -> x0, local copies, waits for them, and re-layouts: 5.92 us -> none  [the longest x6 4.99 us: first(): return (x[:MARGIN], x[:, :MARGIN], x[:MARGIN, :MARGIN])]
    convert_element_type x8 -> x0, other arithmetic: 3.18 us -> none  [the longest x3 2.85 us: scatter_sum(): half = add_up([keep, got]).astype(BF16)]
    select_n x1 -> x2, other arithmetic: 1.26 us -> 4.02 us  [window_labels(): flat = jnp.where(ok, lh * 3 + lw, -1).astype(jnp.int32)]
    squeeze x9 -> x0, local copies, waits for them, and re-layouts: 2.29 us -> none  [the longest x3 2.13 us: scatter_sum(): send = lax.dynamic_index_in_dim(parts, 1 - core, 2, keepdims=False)]
    select_n x1 -> x0, other arithmetic: 2 us -> none  [ahead_index(): return jnp.where(ok, idx, -1).astype(jnp.int32).reshape(-1, 1)]
  transfers between devices with their start and end apart: 41 -> 0, of which waited for: 15 -> 0; matrix products, arithmetic and copies ran while one was open for 18% -> 0% of each run, Pallas kernels for 7% -> 0%
where the time goes in v2:
time: 122 us; the launch traced here: 121 us
  Pallas kernels  89 us (73%)
  local copies, waits for them, and re-layouts  19.6 us (16%)
  other arithmetic  9.43 us (8%)
  between operations  3.26 us (3%)
    pallas_call x1, Pallas kernels, on_device(): pl.pallas_call(functools.partial(whole_kernel, list(inputs), list(outs),...  89 us
    unnamed x7, local copies, waits for them, and re-layouts  7.37 us
    select_n x2, other arithmetic, window_labels(): flat = jnp.where(ok, lh * 3 + lw, -1).astype(jnp.int32)  4.02 us
    reshape x4, local copies, waits for them, and re-layouts, window_labels(): return (flat.reshape(-1, 1), flat.reshape(-1, SLOT))  2.9 us
    reshape x3, local copies, waits for them, and re-layouts, ahead_index(): return jnp.where(ok, idx, -1).astype(jnp.int32).reshape(-1, 1)  2.45 us

profile of v2, /device:TPU:0, one launch (start us, length us, event | category | flops | bytes accessed | tf_op | source)
XLA Modules:
  0.0 121.3 jit_solution(1426329661934472609)
XLA Ops:
  0.6 1.4 %fusion.111 = (s32[1]{0:T(128)}, s32[1]{0:T(128)}, s32[1]{0:T(128)}, s32[1]{0:T(128)}) fusion(s32[4]{0:T(128)} %param.39), kind=kLoop, calls=%fused_computation.185 | loop fusion | bytes 32 | tf_op jit(solution)/shard_map/slice | solution.py:531
  4.6 2.0 %fusion.106 = (s32[128]{0:T(128)S(1)}, s32[128,1]{0,1:T(1,128)S(1)}) fusion(pred[128]{0:T(512)(128)(4,1)} %constant.223.clone, s32[128]{0:T(128)} %constant.222.clone, s32[128]{0:T(128)} %constant.221.clone, s32[]{:T(128)S(6)} %sub.121, s32[]{:T(128)S(6)} %mul.142, s32[]{:T(128)S(6)} %sub.120, s32[]{:T(128)S(6)} %mul.139, s32[]{:T(128)} %bitcast.5, s32[]{:T(128)} %bitcast.4), kind=kLoop, calls=%fused_computation.179 | loop fusion | flops 4096 | bytes 2200 | tf_op jit(solution)/shard_map/jit(_where)/select_n | solution.py:104
  6.6 2.0 %select_bitcast_fusion = s32[112,1]{0,1:T(1,128)S(1)} fusion(pred[112]{0:T(512)(128)(4,1)} %constant.232.clone, s32[112]{0:T(128)} %constant.230.clone, s32[112]{0:T(128)} %constant.231.clone, s32[]{:T(128)} %bitcast.5, s32[]{:T(128)} %bitcast.4), kind=kLoop, calls=%fused_computation.184 | loop fusion | flops 5600 | bytes 1464 | tf_op jit(solution)/shard_map/reshape | solution.py:80
  8.6 0.6 reshape.82.refs_16_
  9.3 2.0 %add_select_fusion.12 = (s32[512]{0:T(512)S(1)}, s32[512]{0:T(512)S(1)}, s32[512]{0:T(512)S(1)}) fusion(pred[512]{0:T(512)(128)(4,1)} %constant.220.clone, s32[512]{0:T(512)} %constant.218.clone, s32[512]{0:T(512)} %constant.219.clone, s32[]{:T(128)S(6)} %sub.119, s32[]{:T(128)S(6)} %mul.138, s32[]{:T(128)S(6)} %sub.118, s32[]{:T(128)S(6)} %mul.135, ...), kind=kLoop, calls=%fused_computation.127 | loop fusion | flops 40448 | bytes 10776 | tf_op jit(solution)/shard_map/jit(_where)/select_n | solution.py:104
  11.3 2.1 %fusion.78 = (s32[448]{0:T(512)S(1)}, s32[448]{0:T(512)S(1)}) fusion(pred[448]{0:T(512)(128)(4,1)} %constant.229.clone, s32[448]{0:T(512)} %constant.228.clone, s32[448]{0:T(512)} %constant.227.clone, s32[]{:T(128)} %bitcast.1, s32[]{:T(128)} %bitcast, pred[448]{0:T(512)(128)(4,1)} %constant.226.clone, s32[448]{0:T(512)} %constant.224.clone, ...), kind=kLoop, calls=%fused_computation.128 | loop fusion | flops 44800 | bytes 11656 | tf_op jit(solution)/shard_map/jit(_where)/select_n | solution.py:80
  13.4 0.7 reshape.80.refs_14_
  14.1 0.7 copy.51.refs_7_
  14.8 0.7 copy.50.refs_5_
  15.5 0.7 copy.55.refs_15_
  16.3 0.8 copy.49.refs_4_
  17.1 0.8 copy.53.refs_10_
  18.0 0.9 copy.52.refs_9_
  18.8 0.8 copy.48.refs_2_
  19.7 0.8 copy.54.refs_13_
  20.5 89.0 %block.1 = (bf16[7,14,512]{2,1,0:T(8,128)(2,1)}, bf16[14,28,256]{2,1,0:T(8,128)(2,1)}, f32[1,1792]{1,0:T(1,128)}, bf16[32,2048]{1,0:T(8,128)(2,1)}, bf16[64,512]{1,0:T(8,128)(2,1)}, /*index=5*/bf16[16,1024]{1,0:T(8,128)(2,1)}) custom-call(bf16[14,28,256]{2,1,0:T(8,128)(2,1)} %refs_0_.1, bf16[7,14,512]{2,1,0:T(8,128)(2,1)} %refs_1_.1, ...), custom_call_target="tpu_custom_call" | custom-call | tf_op jit(solution)/shard_map/block/pallas_call | solution.py:611
  109.5 1.3 %reduce = f32[1792]{0:T(1024)} reduce(f32[1,1792]{1,0:T(1,128)} %get-tuple-element.16, f32[]{:T(128)} %constant.240), dimensions={0}, to_apply=%get-tuple-element.16.reduce_sub_computation | reduce | bytes 14340 | tf_op jit(solution)/shard_map/block/pallas_call | solution.py:611
  110.8 0.7 slice_bitcast_fusion.1
  111.5 0.7 slice.28
  112.2 0.7 reshape.87
  112.9 0.6 copy.56
  113.5 0.8 slice_bitcast_fusion
  114.3 0.9 slice.30
  115.2 0.8 reshape.90
  115.9 0.6 copy.58
  116.6 1.5 %copy.57 = bf16[8,4,8,128]{3,1,2,0:T(4,128)(2,1)} copy(bf16[8,4,8,128]{3,2,1,0:T(8,128)(2,1)} %bitcast.25) | data formatting | bytes 131072
  118.1 1.6 %copy.61 = bf16[7,14,512]{2,1,0:T(8,128)(2,1)} copy(bf16[7,14,512]{2,1,0:T(8,128)(2,1)} %get-tuple-element.39) | data formatting | bytes 200704
  119.6 1.6 %copy.62 = bf16[14,28,256]{2,1,0:T(8,128)(2,1)} copy(bf16[14,28,256]{2,1,0:T(8,128)(2,1)} %get-tuple-element.40) | data formatting | bytes 401408

commit v3 on v2

--- a/solution.py
+++ b/solution.py
@@ -50,34 +50,48 @@
     return h, w, np.tile(ok, 4)
 
 
+def by_window(x):
+    return (x * 9363) >> 16
+
+
 def win_index(h, w, cols):
-    return ((h // WIN) * (cols // WIN) + w // WIN) * SLOT + (h % WIN) * WIN + w % WIN
+    hq, wq = by_window(h), by_window(w)
+    return (hq * (cols // WIN) + wq) * SLOT + (h - hq * WIN) * WIN + w - wq * WIN
 
 
 def quad_index(h, w, rows, cols):
     pitch = pitch_of(cols // 2)
-    return ((h % 2) + 2 * (w % 2)) * ((rows // 2) * pitch) + (h // 2) * pitch + w // 2
-
-
-def ahead_index(h, w, ok, shift_rows, shift_cols, rows, cols, inner, base):
+    return ((h & 1) + 2 * (w & 1)) * ((rows // 2) * pitch) + (h >> 1) * pitch + (w >> 1)
+
+
+def coded(tokens):
+    h, w, ok = tokens
+    return np.where(ok, h * 4096 + w, -1).astype(np.int32).reshape(-1, 1)
+
+
+def decoded(code):
+    return code >> 12, code & 4095, code >= 0
+
+
+def ahead_index(code, shift_rows, shift_cols, rows, cols, inner, base):
+    h, w, ok = decoded(code)
     pitch = pitch_of(cols)
     h2, w2 = h + shift_rows, w + shift_cols
     local = inner(jnp.minimum(h2, rows - 1), jnp.minimum(w2, cols - 1))
     below = base + (h2 - rows) * pitch + w2
     side = base + MARGIN * pitch + h2 * PM + (w2 - cols)
-    idx = jnp.where(w2 >= cols, side, jnp.where(h2 >= rows, below, local))
-    return jnp.where(ok, idx, -1).astype(jnp.int32).reshape(-1, 1)
-
-
-def behind_index(h, w, ok, shift_rows, shift_cols, rows, cols, base):
+    return jnp.where(ok, jnp.where(w2 >= cols, side, jnp.where(h2 >= rows, below, local)), -1)
+
+
+def behind_index(code, shift_rows, shift_cols, rows, cols, base):
+    h, w, ok = decoded(code)
     pitch = pitch_of(cols)
     h2, w2 = h - shift_rows, w - shift_cols
     local = win_index(jnp.maximum(h2, 0), jnp.maximum(w2, 0), cols)
     above = base + (h2 + MARGIN) * pitch + w2
     row = jnp.where(h2 >= 0, h2, rows + h2 + MARGIN)
     side = base + MARGIN * pitch + row * PM + (w2 + MARGIN)
-    idx = jnp.where(w2 < 0, side, jnp.where(h2 < 0, above, local))
-    return jnp.where(ok, idx, -1).astype(jnp.int32).reshape(-1, 1)
+    return jnp.where(ok, jnp.where(w2 < 0, side, jnp.where(h2 < 0, above, local)), -1)
 
 
 def piece_index(rows, cols, inner, first):
@@ -93,16 +107,15 @@
     return np.concatenate(parts).astype(np.int32).reshape(-1, 1)
 
 
-def window_labels(rows, cols, axis_row, axis_col, shift_rows, shift_cols):
-    h, w, ok = window_tokens(rows, cols)
+def window_labels(code, rows, cols, axis_row, axis_col, shift_rows, shift_cols):
+    h, w, ok = decoded(code)
     height = rows * lax.axis_size("rows")
     breadth = cols * lax.axis_size("cols")
     gh = axis_row * rows + h
     gw = axis_col * cols + w
     lh = jnp.where(gh < height - WIN, 0, jnp.where(gh < height - shift_rows, 1, 2))
     lw = jnp.where(gw < breadth - WIN, 0, jnp.where(gw < breadth - shift_cols, 1, 2))
-    flat = jnp.where(ok, lh * 3 + lw, -1).astype(jnp.int32)
-    return flat.reshape(-1, 1), flat.reshape(-1, SLOT)
+    return jnp.where(ok, lh * 3 + lw, -1)
 
 
 def dot(a, b):
@@ -117,11 +130,17 @@
     return lax.dot_general(a, b, (((0,), (0,)), ((), ())), preferred_element_type=F32)
 
 
+def one_hot(idx, count):
+    lane = lax.broadcasted_iota(jnp.int32, (idx.shape[0], count), 1)
+    return jnp.where(idx == lane, 1.0, 0.0).astype(BF16)
+
+
+def picked(hot, source):
+    return dot(hot, source).astype(BF16)
+
+
 def select(idx, source):
-    count = source.shape[0]
-    lane = lax.broadcasted_iota(jnp.int32, (idx.shape[0], count), 1)
-    hot = jnp.where(idx == lane, 1.0, 0.0).astype(BF16)
-    return dot(hot, source).astype(BF16)
+    return picked(one_hot(idx, source.shape[0]), source)
 
 
 def norm_parts(x):
@@ -254,9 +273,14 @@
         self.links, self.kind, self.parts = links, kind, parts
         self.got1, self.half, self.got2, self.part, self.got3 = bufs
 
-    def first(self):
+        self.copies = []
+
+    def first(self, chips=None):
         k = self.links
-        self.copies = [k.start(self.parts.at[1 - k.core], self.got1, k.partner())]
+        for x in range(k.chips) if chips is None else chips:
+            self.copies.append(
+                k.start(self.parts.at[1 - k.core, x], self.got1.at[x], k.partner())
+            )
 
     def second(self):
         k = self.links
@@ -371,6 +395,15 @@
     halos = [[getattr(b, f"h{n}_{i}") for i in range(3)] for n in range(7)]
     margin2 = slice(0, MARGIN * PM)
     masks = head_masks()
+    s0, s1, s2, s3 = (b.shifts[i] for i in range(4))
+    quads, quad_pitch = b.quad.shape[0], pitch_of(cols // 2)
+    n2, n3 = b.win2.shape[0], b.win3.shape[0]
+    base, base3 = rows * pitch, rows3 * pitch3
+    as_grid = lambda h, w: h * pitch + w
+    as_grid3 = lambda h, w: h * pitch3 + w
+    as_quad = lambda h, w: quad_index(h, w, rows, cols)
+    extra = MARGIN * pitch + (rows + MARGIN) * PM
+    extra3 = MARGIN * pitch3 + (rows3 + MARGIN) * PM
 
     b.toks[...] = jnp.zeros_like(b.toks)
     fill_tile(b.toks, b.tok, pitch)
@@ -386,9 +419,17 @@
         b.cots.at[0 : MARGIN * pitch3], b.cside, b.cside.at[margin2], halos[1], -1
     )
 
+    place2 = (rows, cols, links.row, links.col, s0, s1)
+    place3 = (rows3, cols3, links.row, links.col, s2, s3)
+    b.lc2[...] = window_labels(b.win2[...], *place2)
+    b.lr2[...] = window_labels(b.rwin2[...], *place2)
+    b.lc3[...] = window_labels(b.win3[...], *place3)
+    b.lr3[...] = window_labels(b.rwin3[...], *place3)
     quad = select(b.idx_q[...], b.toks[...])
+    idx = ahead_index(b.win2[...], s0, s1, rows, cols, as_grid, base)
+    hot = one_hot(idx, base + extra)
     wait_all(flying)
-    hat, _ = norm_parts(select(b.idx_a[...], joined_ext(b.toks[...], halos[0])).astype(F32))
+    hat, _ = norm_parts(picked(hot, joined_ext(b.toks[...], halos[0])).astype(F32))
     b.rolled[...] = (hat * b.gain2[...]).astype(BF16)
     b.packed[...] = dot(b.rolled[...], b.qkv2[...]).astype(BF16)
     for w in range(b.lr2.shape[0]):
@@ -404,8 +445,9 @@
     last2 = slice((rows - MARGIN) * PM, rows * PM)
     flying = links.exchange(b.row1, b.col1, b.col1.at[last2], halos[2], 1)
 
+    hot = one_hot(behind_index(b.quad[...], s0, s1, rows, cols, n2), n2 + extra)
     wait_all(flying)
-    restored = select(b.idx_c[...], joined_ext(win, halos[2]))
+    restored = picked(hot, joined_ext(win, halos[2]))
     section = (quad.astype(F32) + restored.astype(F32)).astype(BF16)
     t3 = rows3 * pitch3
     joined = jnp.concatenate([section[k * t3 : (k + 1) * t3] for k in range(4)], axis=1)
@@ -423,10 +465,12 @@
     )
 
     wait_all(flying_c)
-    dproj = select(b.idx_d[...], joined_ext(b.cots[...], halos[1]))
+    idx = ahead_index(b.win3[...], s2, s3, rows3, cols3, as_grid3, base3)
+    hot = one_hot(idx, base3 + extra3)
+    dproj = picked(hot, joined_ext(b.cots[...], halos[1]))
     dmixed = dot_nt(dproj, b.proj3[...]).astype(BF16)
     wait_all(flying)
-    rolled3 = select(b.idx_d[...], joined_ext(b.normed3[...], halos[3]))
+    rolled3 = picked(hot, joined_ext(b.normed3[...], halos[3]))
     b.packed3[...] = dot(rolled3, b.qkv3[...]).astype(BF16)
     for w in range(b.lr3.shape[0]):
         bias = window_bias(b.lc3, b.lr3, w)
@@ -448,10 +492,11 @@
     flying = links.exchange(b.row2, b.col2, b.col2.at[last3], halos[4], 1)
     store_parts(b.g3, dot_tn(rolled3, b.dpacked3[...]), 0)
     store_parts(b.g3, dot_tn(b.mixed3[...], dproj), 3 * wide)
-    red3.first()
-
+    red3.first(range(links.chips // 2))
+
+    hot = one_hot(behind_index(b.grid3[...], s2, s3, rows3, cols3, n3), n3 + extra3)
     wait_all(flying)
-    back = select(b.idx_f[...], joined_ext(b.both[...], halos[4]))
+    back = picked(hot, joined_ext(b.both[...], halos[4]))
     mine = b.merged[...].astype(F32)
     total = (mine + back[:, :wide].astype(F32)).astype(BF16)
     for r in range(rows3):
@@ -469,14 +514,18 @@
     )
     put_pieces(b.idx_g, b.dsec[...], b.row3, b.col3)
     flying = links.exchange(b.row3, b.col3, b.col3.at[margin2], halos[5], -1)
+    red3.first(range(links.chips // 2, links.chips))
     store_parts(b.gm, dot_tn(b.mnorm[...], dmerged), 0)
     redm.first()
 
+    idx = ahead_index(b.win2[...], s0, s1, rows, cols, as_quad, quads)
+    hot = one_hot(idx, quads + extra)
     wait_all(flying)
-    red3.second()
-    dproj = select(b.idx_h[...], joined_ext(b.dsec[...], halos[5]))
+    dproj = picked(hot, joined_ext(b.dsec[...], halos[5]))
     dmixed = dot_nt(dproj, b.proj2[...]).astype(BF16)
     for w in range(b.lr2.shape[0]):
+        if w == b.lr2.shape[0] // 2:
+            red3.second()
         bias = window_bias(b.lc2, b.lr2, w)
         at = slice(w * SLOT, (w + 1) * SLOT)
         for g in range(narrow // LANES):
@@ -498,8 +547,9 @@
     red3.third()
     redm.second()
 
+    hot = one_hot(behind_index(b.nat[...], s0, s1, rows, cols, n2), n2 + extra)
     wait_all(flying)
-    dnormed = select(b.idx_i[...], joined_ext(drolled, halos[6])).astype(F32)
+    dnormed = picked(hot, joined_ext(drolled, halos[6])).astype(F32)
     hat, inv = norm_parts(b.toks[...].astype(F32))
     dtok, grad2 = norm_back(hat, inv, b.gain2[...], dnormed)
     b.gg_0[:, :narrow] = grad2
@@ -518,6 +568,25 @@
     b.gains[...] = redg.finish()
 
 
+def finish_kernel(out, dtok, gains, sum3, summ, sum2, o_out, o_dtok, o_gains, *rest):
+    o_out[...] = out[...]
+    o_dtok[...] = dtok[...]
+    for j in range(o_gains.shape[0]):
+        o_gains[j : j + 1, :] = gains[:, j * LANES : (j + 1) * LANES]
+    flats, rooms = rest[: len(rest) // 2], rest[len(rest) // 2 :]
+    wide, narrow = sum3.shape[1] // 4, sum2.shape[1] // 4
+    views = (
+        (sum2, 0, 3 * narrow), (sum2, 3 * narrow, narrow), (summ, 0, wide),
+        (sum3, 0, 3 * wide), (sum3, 3 * wide, wide),
+    )
+    for (source, offset, width), flat, room in zip(views, flats, rooms, strict=True):
+        steps = width // LANES
+        for j in range(steps):
+            piece = source[:, offset + j * LANES : offset + (j + 1) * LANES]
+            room[pl.ds(j, source.shape[0], stride=steps), :] = piece.astype(F32)
+        flat[...] = room[...].astype(BF16)
+
+
 def on_device(
     tokens, cotangent, shifts, norm2_gain, qkv2, proj2, merge_gain, merge_weight, norm3_gain,
     qkv3, proj3,
@@ -527,42 +596,31 @@
     rows3, cols3 = rows // 2, cols // 2
     pitch, pitch3 = pitch_of(cols), pitch_of(cols3)
     base, base3 = rows * pitch, rows3 * pitch3
-    r, c = lax.axis_index("rows"), lax.axis_index("cols")
-    s0, s1, s2, s3 = shifts[0], shifts[1], shifts[2], shifts[3]
-
     win2, win3 = window_tokens(rows, cols), window_tokens(rows3, cols3)
     n2, n3 = len(win2[0]), len(win3[0])
     quad = quad_tokens(rows, cols)
     nat = grid_tokens(rows, cols, pitch)
     grid3 = grid_tokens(rows3, cols3, pitch3)
     as_grid = lambda h, w: h * pitch + w
-    as_grid3 = lambda h, w: h * pitch3 + w
     as_quad = lambda h, w: quad_index(h, w, rows, cols)
     as_win = lambda h, w: win_index(h, w, cols)
     as_win3 = lambda h, w: win_index(h, w, cols3)
     fixed = lambda t, inner: np.where(t[2], inner(t[0], t[1]), -1).astype(np.int32).reshape(-1, 1)
 
-    idx_a = ahead_index(*win2, s0, s1, rows, cols, as_grid, base)
-    idx_h = ahead_index(*win2, s0, s1, rows, cols, as_quad, len(quad[0]))
-    idx_d = ahead_index(*win3, s2, s3, rows3, cols3, as_grid3, base3)
-    idx_c = behind_index(*quad, s0, s1, rows, cols, n2)
-    idx_i = behind_index(*nat, s0, s1, rows, cols, n2)
-    idx_f = behind_index(*grid3, s2, s3, rows3, cols3, n3)
     idx_q = fixed(quad, as_grid)
     idx_n = fixed(nat, as_quad)
     idx_b = piece_index(rows, cols, as_win, False)
     idx_e = piece_index(rows3, cols3, as_win3, False)
     idx_g = piece_index(rows, cols, as_quad, True)
-    lc2, lr2 = window_labels(rows, cols, r, c, s0, s1)
-    lc3, lr3 = window_labels(rows3, cols3, r, c, s2, s3)
     gain2, gainm, gain3 = (g.reshape(1, -1) for g in (norm2_gain, merge_gain, norm3_gain))
     nr, nc = lax.axis_size("rows"), lax.axis_size("cols")
     chips = nc // 2
     quads, gains = len(quad[0]), 5 * narrow + wide
     inputs = dict(
-        tok=tokens, cot=cotangent, idx_a=idx_a, idx_b=idx_b, idx_c=idx_c, idx_d=idx_d, idx_e=idx_e,
-        idx_f=idx_f, idx_g=idx_g, idx_h=idx_h, idx_i=idx_i, idx_n=idx_n, idx_q=idx_q, lc2=lc2,
-        lr2=lr2, lc3=lc3, lr3=lr3, gain2=gain2, gainm=gainm, gain3=gain3, qkv2=qkv2, proj2=proj2,
+        tok=tokens, cot=cotangent, shifts=shifts, win2=coded(win2), win3=coded(win3),
+        rwin2=coded(win2).reshape(-1, SLOT), rwin3=coded(win3).reshape(-1, SLOT),
+        quad=coded(quad), nat=coded(nat), grid3=coded(grid3), idx_b=idx_b, idx_e=idx_e,
+        idx_g=idx_g, idx_n=idx_n, idx_q=idx_q, gain2=gain2, gainm=gainm, gain3=gain3, qkv2=qkv2, proj2=proj2,
         weight=merge_weight, qkv3=qkv3, proj3=proj3,
     )
     m3, mm, m2 = wide // (nr * nc), 4 * narrow // (nr * nc), narrow // (nr * nc)
@@ -590,6 +648,8 @@
         row3=((row2, narrow), BF16), col3=((col2, narrow), BF16),
         row4=((row2, narrow), BF16), col4=((col2, narrow), BF16),
     )
+    ints = dict(lc2=(n2, 1), lr2=(n2 // SLOT, SLOT), lc3=(n3, 1), lr3=(n3 // SLOT, SLOT))
+    scratch |= {name: (shape, jnp.int32) for name, shape in ints.items()}
     copies = 7 * 3
     for n, (big, width) in enumerate(
         ((1, narrow), (0, wide), (1, narrow), (0, wide), (0, 2 * wide), (1, narrow), (1, narrow))
@@ -602,18 +662,21 @@
             ((chips, nr), (chips, nr), (max(chips - 1, 1), nr), (nr,), (max(nr - 1, 1),))
         ):
             scratch[f"{name}_{i}"] = (lead + shape, BF16)
-        copies += chips + nr - 1
+        copies += 2 * chips + nr - 2
     for i, lead in enumerate(((), (), (), (max(chips - 1, 1),), (), (max(nr - 1, 1),))):
         scratch[f"gg_{i}"] = (lead + (1, gains), F32)
     copies += chips + nr - 1
     spaces = [pltpu.VMEM(s, d) for s, d in scratch.values()]
     spaces += [pltpu.SemaphoreType.DMA((copies,)), pltpu.SemaphoreType.DMA((copies,))]
-    out, tokens_grad, total, sum3, sum_m, sum2 = pl.pallas_call(
+    results = pl.pallas_call(
         functools.partial(
             whole_kernel, list(inputs), list(outs), list(scratch) + ["send", "recv"]
         ),
         out_shape=[jax.ShapeDtypeStruct(s, d) for s, d in outs.values()],
-        in_specs=[pl.BlockSpec(memory_space=pltpu.VMEM)] * len(inputs),
+        in_specs=[
+            pl.BlockSpec(memory_space=pltpu.SMEM if name == "shifts" else pltpu.VMEM)
+            for name in inputs
+        ],
         out_specs=[pl.BlockSpec(memory_space=pltpu.VMEM)] * len(outs),
         scratch_shapes=spaces,
         compiler_params=pltpu.CompilerParams(
@@ -621,16 +684,24 @@
         ),
         name="block",
     )(*inputs.values())
-    return (
-        out,
-        tokens_grad,
-        total.reshape(-1),
-        sum2[:, : 3 * narrow].reshape(-1),
-        sum2[:, 3 * narrow :].reshape(-1),
-        sum_m.reshape(-1),
-        sum3[:, : 3 * wide].reshape(-1),
-        sum3[:, 3 * wide :].reshape(-1),
-    )
+    flats = [
+        (m * width // LANES, LANES)
+        for m, width in (
+            (m2, 3 * narrow), (m2, narrow), (mm, wide), (m3, 3 * wide), (m3, wide)
+        )
+    ]
+    final = pl.pallas_call(
+        finish_kernel,
+        out_shape=[
+            jax.ShapeDtypeStruct(cotangent.shape, BF16),
+            jax.ShapeDtypeStruct(tokens.shape, BF16),
+            jax.ShapeDtypeStruct((gains // LANES, LANES), F32),
+        ]
+        + [jax.ShapeDtypeStruct(shape, BF16) for shape in flats],
+        scratch_shapes=[pltpu.VMEM(shape, F32) for shape in flats],
+        name="finish",
+    )(*results)
+    return tuple(final[:2]) + tuple(x.reshape(-1) for x in final[2:])
 
 
 def solution(mesh):

time: 122 us -> 95.4 us (0.78)
  local copies, waits for them, and re-layouts: 19.6 us -> 0 us
  other arithmetic: 9.43 us -> 0 us
  Pallas kernels: 89 us -> 94.5 us
  between operations: 3.26 us -> 0.76 us
    reshape x12 -> x0, local copies, waits for them, and re-layouts: 9.19 us -> none  [the longest x4 2.9 us: window_labels(): return (flat.reshape(-1, 1), flat.reshape(-1, SLOT))]
    unnamed x7 -> x0, local copies, waits for them, and re-layouts: 7.37 us -> none
    select_n x3 -> x0, other arithmetic: 6.11 us -> none  [the longest x2 4.02 us: window_labels(): flat = jnp.where(ok, lh * 3 + lw, -1).astype(jnp.int32)]
    pallas_call x1, Pallas kernels: 89 us -> 92.6 us  [on_device(): pl.pallas_call(functools.partial(whole_kernel, list(inputs), list(outs),...]
    slice x3 -> x0, local copies, waits for them, and re-layouts: 3.03 us -> none  [the longest x1 1.4 us: on_device(): s0, s1, s2, s3 = (shifts[0], shifts[1], shifts[2], shifts[3])]
    reshape x1 -> x0, other arithmetic: 2.01 us -> none  [behind_index(): return jnp.where(ok, idx, -1).astype(jnp.int32).reshape(-1, 1)]
    pallas_call x0 -> x1, Pallas kernels: none -> 1.91 us  [on_device(): pl.pallas_call(finish_kernel, out_shape=[jax.ShapeDtypeStruct(cotangent.s...]
    pallas_call x1 -> x0, other arithmetic: 1.31 us -> none  [on_device(): pl.pallas_call(functools.partial(whole_kernel, list(inputs), list(outs),...]
where the time goes in v3:
time: 95.4 us; the launch traced here: 95.3 us
  Pallas kernels  94.5 us (99%)
    pallas_call x1, Pallas kernels, on_device(): pl.pallas_call(functools.partial(whole_kernel, list(inputs), list(outs),...  92.6 us

profile of v3, /device:TPU:0, one launch (start us, length us, event | category | flops | bytes accessed | tf_op | source)
XLA Modules:
  0.0 95.3 jit_solution(10388863523770500483)
XLA Ops:
  0.6 92.6 %block.1 = (bf16[7,14,512]{2,1,0:T(8,128)(2,1)}, bf16[14,28,256]{2,1,0:T(8,128)(2,1)}, f32[1,1792]{1,0:T(1,128)}, bf16[32,2048]{1,0:T(8,128)(2,1)}, bf16[64,512]{1,0:T(8,128)(2,1)}, /*index=5*/bf16[16,1024]{1,0:T(8,128)(2,1)}) custom-call(bf16[14,28,256]{2,1,0:T(8,128)(2,1)} %refs_0_.1, bf16[7,14,512]{2,1,0:T(8,128)(2,1)} %refs_1_.1, s32[4]{0:T(128)} %refs_2_.1, ...), custom_call_target="tpu_custom_call" | custom-call | tf_op jit(solution)/shard_map/block/pallas_call | solution.py:671
  93.3 1.9 %finish.1 = (bf16[7,14,512]{2,1,0:T(8,128)(2,1)}, bf16[14,28,256]{2,1,0:T(8,128)(2,1)}, f32[14,128]{1,0:T(8,128)}, bf16[96,128]{1,0:T(8,128)(2,1)}, bf16[32,128]...) custom-call(bf16[7,14,512]{2,1,0:T(8,128)(2,1)} %get-tuple-element.22.out, ...), custom_call_target="tpu_custom_call" | custom-call | tf_op jit(solution)/shard_map/finish/pallas_call | solution.py:693

commit v4 on v3

--- a/solution.py
+++ b/solution.py
@@ -273,32 +273,36 @@
         self.links, self.kind, self.parts = links, kind, parts
         self.got1, self.half, self.got2, self.part, self.got3 = bufs
 
-        self.copies = []
-
-    def first(self, chips=None):
+
+    def start_first(self, d):
         k = self.links
-        for x in range(k.chips) if chips is None else chips:
-            self.copies.append(
-                k.start(self.parts.at[1 - k.core, x], self.got1.at[x], k.partner())
-            )
+        x = lax.rem(k.chip + d, k.chips)
+        return k.start(self.parts.at[1 - k.core, x], self.got1.at[x], k.partner())
+
+    def first_away(self):
+        self.away = [self.start_first(d) for d in range(1, self.links.chips)]
+
+    def first_own(self):
+        self.own = self.start_first(0)
+
+    def both_cores(self, x, r):
+        return self.parts[self.links.core, x, r].astype(F32) + self.got1[x, r].astype(F32)
 
     def second(self):
         k = self.links
-        wait_all(self.copies)
-        for x in range(k.chips):
+        wait_all(self.away)
+        self.copies = []
+        for d in range(1, k.chips):
+            x = lax.rem(k.chip + d, k.chips)
             for r in range(k.nr):
-                total = self.parts[k.core, x, r].astype(F32) + self.got1[x, r].astype(F32)
-                self.half[x, r] = total.astype(self.kind)
-        self.copies = [
-            k.start(self.half.at[lax.rem(k.chip + d, k.chips)], self.got2.at[d - 1], k.device(0, 2 * d))
-            for d in range(1, k.chips)
-        ]
+                self.half[x, r] = self.both_cores(x, r).astype(self.kind)
+            self.copies.append(k.start(self.half.at[x], self.got2.at[d - 1], k.device(0, 2 * d)))
 
     def third(self):
         k = self.links
-        wait_all(self.copies)
+        wait_all([self.own] + self.copies)
         for r in range(k.nr):
-            total = self.half[k.chip, r].astype(F32)
+            total = self.both_cores(k.chip, r)
             for d in range(1, k.chips):
                 total = total + self.got2[d - 1, r].astype(F32)
             self.part[r] = total.astype(self.kind)
@@ -492,7 +496,7 @@
     flying = links.exchange(b.row2, b.col2, b.col2.at[last3], halos[4], 1)
     store_parts(b.g3, dot_tn(rolled3, b.dpacked3[...]), 0)
     store_parts(b.g3, dot_tn(b.mixed3[...], dproj), 3 * wide)
-    red3.first(range(links.chips // 2))
+    red3.first_away()
 
     hot = one_hot(behind_index(b.grid3[...], s2, s3, rows3, cols3, n3), n3 + extra3)
     wait_all(flying)
@@ -514,9 +518,11 @@
     )
     put_pieces(b.idx_g, b.dsec[...], b.row3, b.col3)
     flying = links.exchange(b.row3, b.col3, b.col3.at[margin2], halos[5], -1)
-    red3.first(range(links.chips // 2, links.chips))
+    red3.first_own()
     store_parts(b.gm, dot_tn(b.mnorm[...], dmerged), 0)
-    redm.first()
+    redm.first_away()
+    redm.first_own()
+    red3.second()
 
     idx = ahead_index(b.win2[...], s0, s1, rows, cols, as_quad, quads)
     hot = one_hot(idx, quads + extra)
@@ -524,8 +530,6 @@
     dproj = picked(hot, joined_ext(b.dsec[...], halos[5]))
     dmixed = dot_nt(dproj, b.proj2[...]).astype(BF16)
     for w in range(b.lr2.shape[0]):
-        if w == b.lr2.shape[0] // 2:
-            red3.second()
         bias = window_bias(b.lc2, b.lr2, w)
         at = slice(w * SLOT, (w + 1) * SLOT)
         for g in range(narrow // LANES):
@@ -543,7 +547,8 @@
     flying = links.exchange(b.row4, b.col4, b.col4.at[last2], halos[6], 1)
     store_parts(b.g2, dot_tn(b.rolled[...], b.dpacked[...]), 0)
     store_parts(b.g2, dot_tn(b.mixed[...], dproj), 3 * narrow)
-    red2.first()
+    red2.first_away()
+    red2.first_own()
     red3.third()
     redm.second()
 

time: 95.4 us -> 89.6 us (0.939)
  Pallas kernels: 94.5 us -> 88.7 us
    pallas_call x1, Pallas kernels: 92.6 us -> 86.8 us  [on_device(): pl.pallas_call(functools.partial(whole_kernel, list(inputs), list(outs),...]
where the time goes in v4:
time: 89.6 us; the launch traced here: 89.5 us
  Pallas kernels  88.7 us (99%)
    pallas_call x1, Pallas kernels, on_device(): pl.pallas_call(functools.partial(whole_kernel, list(inputs), list(outs),...  86.8 us
    pallas_call x1, Pallas kernels, on_device(): pl.pallas_call(finish_kernel, out_shape=[jax.ShapeDtypeStruct(cotangent.s...  1.91 us

profile of v4, /device:TPU:0, one launch (start us, length us, event | category | flops | bytes accessed | tf_op | source)
XLA Modules:
  0.0 89.5 jit_solution(16114175967027361239)
XLA Ops:
  0.6 86.8 %block.1 = (bf16[7,14,512]{2,1,0:T(8,128)(2,1)}, bf16[14,28,256]{2,1,0:T(8,128)(2,1)}, f32[1,1792]{1,0:T(1,128)}, bf16[32,2048]{1,0:T(8,128)(2,1)}, bf16[64,512]{1,0:T(8,128)(2,1)}, /*index=5*/bf16[16,1024]{1,0:T(8,128)(2,1)}) custom-call(bf16[14,28,256]{2,1,0:T(8,128)(2,1)} %refs_0_.1, bf16[7,14,512]{2,1,0:T(8,128)(2,1)} %refs_1_.1, s32[4]{0:T(128)} %refs_2_.1, ...), custom_call_target="tpu_custom_call" | custom-call | tf_op jit(solution)/shard_map/block/pallas_call | solution.py:676
  87.4 1.9 %finish.1 = (bf16[7,14,512]{2,1,0:T(8,128)(2,1)}, bf16[14,28,256]{2,1,0:T(8,128)(2,1)}, f32[14,128]{1,0:T(8,128)}, bf16[96,128]{1,0:T(8,128)(2,1)}, bf16[32,128]...) custom-call(bf16[7,14,512]{2,1,0:T(8,128)(2,1)} %get-tuple-element.22.out, ...), custom_call_target="tpu_custom_call" | custom-call | tf_op jit(solution)/shard_map/finish/pallas_call | solution.py:698
